TPU v7x, 256 devices: a whole 4x4x8 slice. The times are simulated.
256 devices in a mesh: dp: 64 (over y, x, z_lo), mp: 4 (over z_hi, core).
Axes of the slice: x: 4, y: 4, z: 8 (z_hi: 2, z_lo: 4; z = z_hi * 4 + z_lo), core: 2. Of those that a mesh axis runs over, the one named last changes fastest.
Arguments:
- act_in: bfloat16 [8192, 4096], P('dp', 'mp'), may hold values from -6 to 6
- grad_in: bfloat16 [8192, 16384], P('dp'), may hold values from -6 to 6
- query_act: bfloat16 [1024, 4096], P('dp', 'mp'), may hold values from -6 to 6
- query_grad: bfloat16 [1024, 16384], P('dp'), may hold values from -6 to 6
- act_basis: bfloat16 [4096, 128], P('mp'), may hold values from -1.1 to 1.1
- grad_basis: bfloat16 [16384, 128], P('dp'), may hold values from -1.1 to 1.1
- seq_lengths: int32 [4], replicated, may hold values from 1 to 2048, 6144 in all
Outputs:
- moments: float32 [4096, 16384], P('mp', 'dp')
- scores: float32 [64, 4], replicated
Inputs may be any that keep to these rules, and one draw needn't show every extreme that they name: `seq_lengths`: live tokens are the first ones of each sequence, and one sequence is full.
All inputs are finite; a program needn't handle non-finite values.
Results may differ from a plain program's by a relative error of at most 0.0046.
Values may be sent and summed in bfloat16 or wider, within the bound.
No kernel may reach another device: no remote copies, remote signals or barrier semaphores. Data moves between devices by JAX's collectives and lax.ppermute only.
A program may use at most 192 MiB of HBM per device.

v0:
```python
import functools
import math

import jax
import jax.numpy as jnp
from jax import lax
from jax.experimental import pallas as pl
from jax.experimental.pallas import tpu as pltpu
from jax.sharding import Mesh
from jax.sharding import PartitionSpec as P

D = 4096
FF = 16384
BLOCK = 128
SEQS = 4
SEQ_LEN = 2048
TOKENS = 8192
QUERIES = 64
QUERY_LEN = 16
QROWS = 1024
RING = 4
TOK = 128
QTOK = 16
ROWS = TOK + QTOK
FEAT = 1024
HALF = 512
COLS = 256
UNIT = 512
KC = 256
PLANE = 16
Y, X, Z, H, C = "dp_0", "dp_1", "dp_2", "mp_0", "mp_1"
DP = (Y, X, Z)
MP = (H, C)
ALL = (Y, X, Z, H, C)
damping = 0.1


VM = pltpu.VMEM
SM = pltpu.SMEM
ANY = pl.ANY


def spec(space):
    return pl.BlockSpec(memory_space=space)


def dot(a, b, da, db):
    return lax.dot_general(
        a, b, (((da,), (db,)), ((), ())), preferred_element_type=jnp.float32
    )


def where():
    return tuple(lax.axis_index(a) for a in (Y, X, Z, H, C))


def rotate_act_kernel(len_ref, act_ref, q_ref, basis_ref, out_ref):
    y, x, z, _, _ = where()
    live = jnp.clip(len_ref[y] - (x * RING + z) * TOK, 0, TOK)
    mask = lax.broadcasted_iota(jnp.int32, (TOK, BLOCK), 0) < live
    for b in range(FEAT // BLOCK):
        cols = pl.ds(b * BLOCK, BLOCK)
        basis = basis_ref[cols, :]
        t = dot(act_ref[:, cols], basis, 1, 0)
        out_ref[0:TOK, cols] = jnp.where(mask, t, 0.0).astype(jnp.bfloat16)
        q = dot(q_ref[:, cols], basis, 1, 0)
        out_ref[TOK:ROWS, cols] = q.astype(jnp.bfloat16)


def rotate_act(lengths, act_in, query_act, act_basis):
    return pl.pallas_call(
        rotate_act_kernel,
        out_shape=jax.ShapeDtypeStruct((ROWS, FEAT), jnp.bfloat16),
        in_specs=[spec(SM), spec(VM), spec(VM), spec(VM)],
        out_specs=spec(VM),
        name="rotate_act",
    )(lengths, act_in, query_act, act_basis)


PART = ROWS // 2
SENT = 2 * ROWS + PART


def pack_kernel(g_ref, q_ref, after_ref, out_ref, sem):
    _, _, z, h, c = where()
    copies = []

    def send(src, dst):
        copies.append(pltpu.make_async_copy(src, dst, sem.at[len(copies)]))

    for n in range(PLANE):

        def cols(step):
            at = n * RING * COLS + lax.rem(z + step, RING) * COLS + c * BLOCK
            return pl.ds(pl.multiple_of(at, BLOCK), BLOCK)

        odd = cols(1 + 2 * h)
        send(g_ref.at[:, cols(0)], out_ref.at[n, pl.ds(0, TOK), :])
        send(q_ref.at[:, cols(0)], out_ref.at[n, pl.ds(TOK, QTOK), :])
        send(g_ref.at[:, odd], out_ref.at[n, pl.ds(ROWS, TOK), :])
        send(q_ref.at[:, odd], out_ref.at[n, pl.ds(ROWS + TOK, QTOK), :])
    for copy in copies:
        copy.start()

    def half(n, pieces):
        at = n * RING * COLS + lax.rem(z + 2, RING) * COLS + c * BLOCK
        cols = pl.ds(pl.multiple_of(at, BLOCK), BLOCK)
        return [
            pltpu.make_async_copy(
                ref.at[rows, cols], out_ref.at[n, to, :], sem.at[4 * PLANE + 2 * n + k]
            )
            for k, (ref, rows, to) in enumerate(pieces)
        ]

    cut = 2 * ROWS + TOK - PART
    halves = (
        ((g_ref, pl.ds(0, PART), pl.ds(2 * ROWS, PART)),),
        (
            (g_ref, pl.ds(PART, TOK - PART), pl.ds(2 * ROWS, TOK - PART)),
            (q_ref, pl.ds(0, QTOK), pl.ds(cut, QTOK)),
        ),
    )
    for k in range(2):

        @pl.when(h == k)
        def _():
            rest = [copy for n in range(PLANE) for copy in half(n, halves[k])]
            for copy in rest:
                copy.start()
            for copy in rest:
                copy.wait()

    for copy in copies:
        copy.wait()


def pack(grad_in, query_grad, after):
    return pl.pallas_call(
        pack_kernel,
        out_shape=jax.ShapeDtypeStruct((PLANE, SENT, BLOCK), jnp.bfloat16),
        in_specs=[spec(ANY)] * 3,
        out_specs=spec(VM),
        scratch_shapes=[pltpu.SemaphoreType.DMA((6 * PLANE,))],
        name="pack",
    )(grad_in, query_grad, after)


def rotate_grad_kernel(own_ref, u1_ref, u2_ref, f1_ref, f2_ref, basis_ref, out_ref, q_ref, far_ref):
    _, _, z, h, c = where()
    at = pl.multiple_of(c * BLOCK, BLOCK)
    basis_t = basis_ref[pl.ds(at, BLOCK), :].astype(jnp.float32).T.astype(jnp.bfloat16)
    p = h * RING + z
    first = jnp.logical_and(p >= 2, p < 6)

    @pl.when(first)
    def _():
        far_ref[:, 0:PART, :] = f1_ref[...]
        far_ref[:, PART:ROWS, :] = f2_ref[...]

    @pl.when(jnp.logical_not(first))
    def _():
        far_ref[:, 0:PART, :] = f2_ref[...]
        far_ref[:, PART:ROWS, :] = f1_ref[...]

    below = jnp.logical_and(p >= 1, p < 5)
    step = jnp.where(below, 3, 1)
    group = 4
    for ref, s in ((own_ref, 0), (u1_ref, step), (u2_ref, RING - step), (far_ref, 2)):
        src = lax.rem(z + s, RING)

        @pl.loop(0, PLANE // group)
        def _(i):
            rows = ref[pl.ds(i * group, group), 0:TOK, :].reshape(group * TOK, BLOCK)
            t = dot(basis_t, rows, 1, 1).astype(jnp.bfloat16)
            for k in range(group):
                block = (i * group + k) * RING + src
                at = pl.multiple_of(block * TOK, TOK)
                out_ref[:, pl.ds(at, TOK)] = t[:, k * TOK : (k + 1) * TOK]
                at = pl.multiple_of(block * QTOK, QTOK)
                q_ref[pl.ds(at, QTOK), :] = ref[i * group + k, TOK:ROWS, :]

    q = dot(basis_t, q_ref[...], 1, 1)
    out_ref[:, pl.ds(TOKENS, QROWS)] = q.astype(jnp.bfloat16)


def rotate_grad(parts, basis):
    return pl.pallas_call(
        rotate_grad_kernel,
        out_shape=jax.ShapeDtypeStruct((BLOCK, TOKENS + QROWS), jnp.bfloat16),
        in_specs=[spec(VM)] * 6,
        out_specs=spec(VM),
        scratch_shapes=[
            pltpu.VMEM((QROWS, BLOCK), jnp.bfloat16),
            pltpu.VMEM((PLANE, ROWS, BLOCK), jnp.bfloat16),
        ],
        compiler_params=pltpu.CompilerParams(vmem_limit_bytes=16 << 20),
        cost_estimate=pl.CostEstimate(
            flops=2 * (TOKENS + QROWS) * BLOCK * BLOCK,
            bytes_accessed=5 << 20,
            transcendentals=0,
        ),
        name="rotate_grad",
    )(*parts, basis)


def assemble_kernel(*refs):
    ins, outs = refs[:RING], refs[RING:]
    z = lax.axis_index(Z)
    for slot in range(RING):
        zb = lax.rem(z - slot + RING, RING)
        half, odd = zb // 2, lax.rem(zb, 2)
        at = pl.multiple_of(odd * TOK, TOK)
        qat = pl.multiple_of(2 * TOK + odd * QTOK, QTOK)
        for part in range(2):
            cols = pl.ds(part * HALF, HALF)
            outs[part][half, pl.ds(at, TOK), :] = ins[slot][0:TOK, cols]
            outs[part][half, pl.ds(qat, QTOK), :] = ins[slot][TOK:ROWS, cols]


def assemble(blocks):
    unit = jax.ShapeDtypeStruct((2, 2 * ROWS, HALF), jnp.bfloat16)
    return pl.pallas_call(
        assemble_kernel,
        out_shape=(unit, unit),
        in_specs=[spec(VM)] * RING,
        out_specs=(spec(VM), spec(VM)),
        compiler_params=pltpu.CompilerParams(vmem_limit_bytes=8 << 20),
        name="assemble",
    )(*blocks)


def join_kernel(a_ref, b_ref, out_ref, sem):
    copies = [
        pltpu.make_async_copy(ref, out_ref.at[pl.ds(2 * n, 2)], sem.at[n])
        for n, ref in enumerate((a_ref, b_ref))
    ]
    for c in copies:
        c.start()
    for c in copies:
        c.wait()


def join(a, b):
    return pl.pallas_call(
        join_kernel,
        out_shape=jax.ShapeDtypeStruct((4, 2 * ROWS, HALF), jnp.bfloat16),
        in_specs=[spec(ANY)] * 2,
        out_specs=spec(VM),
        scratch_shapes=[pltpu.SemaphoreType.DMA((2,))],
        compiler_params=pltpu.CompilerParams(vmem_limit_bytes=4 << 20),
        name="join",
    )(a, b)


def place(at, slot):
    return lax.rem(at - slot + RING, RING)


HALVES = 2 * RING


def group_copies(part, outer, pair_refs, grad_refs, u_ref, g_ref, sem):
    y, x, _, _, _ = where()
    out = [
        pltpu.make_async_copy(ref, u_ref.at[pl.ds(4 * n, 4)], sem.at[n])
        for n, ref in enumerate(pair_refs)
    ]
    for m, ref in enumerate(grad_refs):
        if part == 0:
            at = pl.multiple_of(place(y, outer) * SEQ_LEN, SEQ_LEN)
            out.append(pltpu.make_async_copy(ref.at[:, pl.ds(at, SEQ_LEN)], g_ref.at[m], sem.at[2 + RING * m]))
            continue
        for s in range(SEQS):
            at = pl.multiple_of(s * SEQ_LEN + place(x, outer) * UNIT, UNIT)
            out.append(pltpu.make_async_copy(ref.at[:, pl.ds(at, UNIT)], g_ref.at[m, :, pl.ds(s * UNIT, UNIT)], sem.at[2 + RING * m + s]))
    return out


SEMS = 2 + 2 * RING


def contract(part, outer, len_ref, u_ref, g_ref, mom_ref, seq_ref, q_ref):
    y, x, _, _, _ = where()

    @pl.loop(0, HALVES)
    def _(n):
        v = place(x if part == 0 else y, n // 2)
        half = lax.rem(n, 2)
        seq, block = (place(y, outer), v) if part == 0 else (v, place(x, outer))
        q_at = v * 64 if part == 0 else v * 256 + block * 64
        q_at = pl.multiple_of(q_at + half * 32, 32)
        q_ref[pl.ds(q_at, 32), :] = u_ref[n, KC : KC + 32, :]

        @pl.when(len_ref[seq] > block * UNIT + half * KC)
        def _():
            at = pl.multiple_of(v * UNIT + half * KC, KC)
            a = u_ref[n, 0:KC, :]
            g = jnp.concatenate([g_ref[0, :, pl.ds(at, KC)], g_ref[1, :, pl.ds(at, KC)]])
            seq_ref[seq if part else 0] += dot(g, a, 1, 0)
            mom_ref[...] += dot(g * g, a * a, 1, 0)


def group_kernel(part, outer, len_ref, mine_ref, other_ref, p_ref, q_ref, *refs):
    carried = 0 if outer == 0 else 2 if part == 0 else 3
    refs = refs[carried:]
    mom_ref, seq_ref, qout_ref, u_ref, g_ref, sem = refs
    copies = group_copies(part, outer, (p_ref, q_ref), (mine_ref, other_ref), u_ref, g_ref, sem)
    for c in copies:
        c.start()
    if not outer:
        mom_ref[...] = jnp.zeros_like(mom_ref)
    if not (outer and part):
        seq_ref[...] = jnp.zeros_like(seq_ref)
    for c in copies:
        c.wait()
    if part == 0:
        y = lax.axis_index(Y)
        row = pl.multiple_of(place(y, outer) * 256, 256)
        qout_ref = qout_ref.at[pl.ds(row, 256), :]
    contract(part, outer, len_ref, u_ref, g_ref, mom_ref, seq_ref, qout_ref)


def group(part, outer, lengths, mine, other, pairs, mom, seqs, queries):
    seq_rows = 1 if part == 0 else SEQS
    carried, alias = [], {}
    if outer:
        carried = [mom, queries] if part == 0 else [mom, seqs, queries]
        alias = {5: 0, 6: 2} if part == 0 else {5: 0, 6: 1, 7: 2}
    return pl.pallas_call(
        functools.partial(group_kernel, part, outer),
        out_shape=(
            jax.ShapeDtypeStruct((COLS, HALF), jnp.float32),
            jax.ShapeDtypeStruct((seq_rows, COLS, HALF), jnp.float32),
            jax.ShapeDtypeStruct((QROWS, HALF), jnp.bfloat16),
        ),
        in_specs=[spec(SM)] + [spec(ANY)] * 4 + [spec(VM)] * len(carried),
        out_specs=(spec(VM),) * 3,
        scratch_shapes=[
            pltpu.VMEM((HALVES, 2 * ROWS, HALF), jnp.bfloat16),
            pltpu.VMEM((2, BLOCK, SEQ_LEN), jnp.bfloat16),
            pltpu.SemaphoreType.DMA((SEMS,)),
        ],
        input_output_aliases=alias,
        compiler_params=pltpu.CompilerParams(vmem_limit_bytes=16 << 20),
        cost_estimate=pl.CostEstimate(
            flops=4 * TOKENS * HALF * COLS // 4,
            bytes_accessed=6 << 20,
            transcendentals=0,
        ),
    )(lengths, mine, other, *pairs, *carried)


FAR = 2


def last_kernel(len_ref, scale_ref, mine_ref, other_ref, *refs):
    pairs, refs = (refs[0:2], refs[2:4]), refs[4:]
    moms, seq_a, seq_b, q_ins, refs = refs[0:2], refs[2:5], refs[5], refs[6:8], refs[8:]
    out_ref, score_ref, w_ref, s_ref, q_ref, u_ref, g_ref, qg_ref, p_ref, sem = refs
    y, _, _, _, c = where()
    copies = []
    for part in range(2):
        copies += group_copies(part, FAR, pairs[part], (mine_ref, other_ref), u_ref.at[part], g_ref.at[part], sem.at[part])
    for m, ref in enumerate((mine_ref, other_ref)):
        copies.append(pltpu.make_async_copy(ref.at[:, pl.ds(TOKENS, QROWS)], qg_ref.at[m], sem.at[2, m]))
    for copy in copies:
        copy.start()
    for part in range(2):
        w_ref[part] = moms[part][...]
        q_ref[part] = q_ins[part][...]
    for n, slot in enumerate((0, 1, 3)):
        s_ref[0, place(y, slot)] = seq_a[n][0]
    far = place(y, FAR)
    s_ref[0, far] = jnp.zeros((COLS, HALF), jnp.float32)
    s_ref[1] = seq_b[...]
    for copy in copies:
        copy.wait()
    row = pl.multiple_of(far * 256, 256)
    contract(0, FAR, len_ref, u_ref.at[0], g_ref.at[0], w_ref.at[0], s_ref.at[0, pl.ds(far, 1)], q_ref.at[0, pl.ds(row, 256), :])
    contract(1, FAR, len_ref, u_ref.at[1], g_ref.at[1], w_ref.at[1], s_ref.at[1], q_ref.at[1])

    mine_at = pl.multiple_of(c * BLOCK, BLOCK)
    other_at = pl.multiple_of((1 - c) * BLOCK, BLOCK)

    @pl.loop(0, FEAT // 256)
    def _(k):
        part, cols = k // 2, pl.ds(pl.multiple_of(lax.rem(k, 2) * 256, 256), 256)
        m = w_ref[part, :, cols] / scale_ref[SEQS]
        rows = pl.ds(pl.multiple_of(k * 256, 256), 256)
        out_ref[rows, pl.ds(mine_at, BLOCK)] = m[0:BLOCK, :].T
        out_ref[rows, pl.ds(other_at, BLOCK)] = m[BLOCK:COLS, :].T
        w_ref[part, :, cols] = 1.0 / (m + damping)

    @pl.loop(0, SEQS)
    def _(s):
        for part in range(2):
            p = w_ref[part] * s_ref[part, s] * scale_ref[s]
            p_ref[part] = p.astype(jnp.bfloat16)

        @pl.loop(0, 2)
        def _(k):
            rows = pl.ds(pl.multiple_of(k * 512, 512), 512)
            mapped = dot(p_ref[0], q_ref[0, rows, :], 1, 1)
            mapped += dot(p_ref[1], q_ref[1, rows, :], 1, 1)
            total = jnp.sum(mapped[0:BLOCK] * qg_ref[0, :, rows].astype(jnp.float32), axis=0, keepdims=True)
            total += jnp.sum(mapped[BLOCK:COLS] * qg_ref[1, :, rows].astype(jnp.float32), axis=0, keepdims=True)
            score_ref[pl.ds(s, 1), rows] = total


def last(lengths, scales, mine, other, pairs, carried):
    return pl.pallas_call(
        last_kernel,
        out_shape=(
            jax.ShapeDtypeStruct((FEAT, COLS), jnp.float32),
            jax.ShapeDtypeStruct((SEQS, QROWS), jnp.float32),
        ),
        in_specs=[spec(SM)] * 2 + [spec(ANY)] * 6 + [spec(VM)] * len(carried),
        out_specs=(spec(VM), spec(VM)),
        scratch_shapes=[
            pltpu.VMEM((2, COLS, HALF), jnp.float32),
            pltpu.VMEM((2, SEQS, COLS, HALF), jnp.float32),
            pltpu.VMEM((2, QROWS, HALF), jnp.bfloat16),
            pltpu.VMEM((2, HALVES, 2 * ROWS, HALF), jnp.bfloat16),
            pltpu.VMEM((2, 2, BLOCK, SEQ_LEN), jnp.bfloat16),
            pltpu.VMEM((2, BLOCK, QROWS), jnp.bfloat16),
            pltpu.VMEM((2, COLS, HALF), jnp.bfloat16),
            pltpu.SemaphoreType.DMA((3, SEMS)),
        ],
        compiler_params=pltpu.CompilerParams(vmem_limit_bytes=32 << 20),
        name="last",
    )(lengths, scales, mine, other, *pairs, *carried)


def shift(x, axis, step):
    return lax.ppermute(x, axis, [(i, (i + step) % RING) for i in range(RING)])


def spread(own, inner_axis, outer_axis, up):
    left = shift(own, inner_axis, 1)
    right = shift(own, inner_axis, -1)
    step, source = (1, left) if up else (-1, right)
    far = shift(source, inner_axis, step)
    pairs = (join(own, left), join(far, right))
    down = [shift(u, outer_axis, 1) for u in pairs]
    up = [shift(u, outer_axis, -1) for u in pairs]
    ends = (shift(down[0], outer_axis, 1), shift(up[1], outer_axis, -1))
    return [pairs, down, ends, up]


def at_z(k):
    k %= 2 * RING
    return k % RING * 2 + k // RING


def along_z(x, pairs):
    return lax.ppermute(x, (Z, H), [(at_z(a), at_z(b)) for a, b in pairs])


ONE = ((0, 1), (1, 2), (2, 3), (3, 4), (4, 7), (5, 0), (6, 5), (7, 6))
TWO = ((0, 5), (1, 6), (2, 7), (3, 0), (4, 3), (5, 4), (6, 1), (7, 2))
UP = tuple((k, k + 2) for k in range(8))
DOWN = tuple((k, k - 2) for k in range(8))


def local(act_in, grad_in, query_act, query_grad, act_basis, grad_basis, seq_lengths):
    own = rotate_act(seq_lengths, act_in, query_act, act_basis)
    blocks = [own] + [shift(own, Z, s) for s in range(1, RING)]

    packed = pack(grad_in, query_grad, own)
    received = lax.all_to_all(packed, (Y, X), 0, 0, tiled=True)
    odd, part = received[:, ROWS : 2 * ROWS], received[:, 2 * ROWS : SENT]
    parts = [received, along_z(odd, ONE), along_z(odd, TWO), along_z(part, UP), along_z(part, DOWN)]
    mine = rotate_grad(parts, grad_basis)
    other = lax.ppermute(mine, C, [(0, 1), (1, 0)])

    part_a, part_b = assemble(blocks)
    pairs = (spread(part_a, X, Y, True), spread(part_b, Y, X, False))
    moms, seqs, queries = [None, None], [[], []], [None, None]
    for outer in (0, 1, 3):
        for part in range(2):
            last_seqs = seqs[part][-1] if outer else None
            moms[part], s, queries[part] = group(part, outer, seq_lengths, mine, other, pairs[part][outer], moms[part], last_seqs, queries[part])
            seqs[part].append(s)

    counted = jnp.sum(seq_lengths).astype(jnp.float32)
    scales = jnp.concatenate(
        [lax.rsqrt(seq_lengths.astype(jnp.float32)), counted[None]]
    )
    carried = [*moms, *seqs[0], seqs[1][-1], *queries]
    far = [*pairs[0][FAR], *pairs[1][FAR]]
    moments, per_row = last(seq_lengths, scales, mine, other, far, carried)
    per_query = jnp.sum(per_row.reshape(SEQS, QUERIES, QUERY_LEN), axis=2)
    partial = per_query.reshape(2, 128) / math.sqrt(QUERY_LEN * D * FF)
    everywhere = jnp.broadcast_to(partial[None], (256, 2, 128))
    scores = lax.all_to_all(everywhere, ALL, 0, 0, tiled=True).sum(0)
    return moments, scores.reshape(SEQS, QUERIES).T


def solution(mesh):
    finer = Mesh(mesh.devices.reshape(4, 4, 4, 2, 2), ALL)
    placed = (P(DP, MP), P(DP, None), P(DP, MP), P(DP, None), P(MP, None), P(DP, None), P())

    return jax.shard_map(
        local, mesh=finer, in_specs=placed, out_specs=(P(MP, DP), P()), check_vma=False
    )
```

profile of v0, /device:TPU:1, one launch (start us, length us, event | category | flops | bytes accessed | tf_op | source)
XLA Modules:
  0.0 271.3 jit_solution(5122511428985331728)
XLA Ops:
  0.6 2.0 rotate_act.1.after_ref.refs_0_
  2.7 3.6 %pack.1 = bf16[16,360,128]{2,1,0:T(8,128)(2,1)} custom-call(bf16[128,16384]{1,0:T(8,128)(2,1)} %g_ref.1, bf16[16,16384]{1,0:T(8,128)(2,1)} %q_ref.3, bf16[144,1024]{1,0:T(8,128)(2,1)} %rotate_act.1.after_ref.refs_0_), custom_call_target="tpu_custom_call" | custom-call | tf_op jit(solution)/shard_map/pack/pallas_call | solution.py:138
  6.3 7.7 %all-to-all-start = ((bf16[16,360,128]{2,1,0:T(8,128)(2,1)}), bf16[16,360,128]{2,1,0:T(8,128)(2,1)S(1)}, u32[]{:S(2)}, u32[]{:S(2)}) async-start(bf16[16,360,128]{2,1,0:T(8,128)(2,1)} %pack.1), calls=%async_computation | async-start | bytes 2949120 | tf_op jit(solution)/shard_map/all_to_all | solution.py:470
  14.0 1.7 collective-permute-start.5
  15.7 3.0 %collective-permute-start.6 = (bf16[144,1024]{1,0:T(8,128)(2,1)S(1)}, bf16[144,1024]{1,0:T(8,128)(2,1)S(1)}, u32[]{:S(2)}, u32[]{:S(2)}) collective-permute-start(bf16[144,1024]{1,0:T(8,128)(2,1)S(1)} %copy-done.11), channel_id=1, source_target_pairs={{0,8},{4,12},{8,0},{12,4},{1,9},{5,13},{9,1},{13,5},{2,10},{6,14},... | collective-permute-start | bytes 884744 | tf_op jit(solution)/shard_map/ppermute | solution.py:435
  19.4 5.5 %collective-permute-done.5.refs_1_ = bf16[144,1024]{1,0:T(8,128)(2,1)S(1)} collective-permute-done((bf16[144,1024]{1,0:T(8,128)(2,1)S(1)}, bf16[144,1024]{1,0:T(8,128)(2,1)S(1)}, u32[]{:S(2)}, u32[]{:S(2)}) %collective-permute-start.5) | collective-permute-done | bytes 294944 | tf_op jit(solution)/shard_map/ppermute | solution.py:435
  24.9 13.6 %collective-permute-done.6.refs_2_ = bf16[144,1024]{1,0:T(8,128)(2,1)S(1)} collective-permute-done((bf16[144,1024]{1,0:T(8,128)(2,1)S(1)}, bf16[144,1024]{1,0:T(8,128)(2,1)S(1)}, u32[]{:S(2)}, u32[]{:S(2)}) %collective-permute-start.6) | collective-permute-done | bytes 294944 | tf_op jit(solution)/shard_map/ppermute | solution.py:435
  39.5 2.6 collective-permute-start.18
  43.3 6.7 %collective-permute-start = (bf16[16,144,128]{2,1,0:T(8,128)(2,1)S(1)}, bf16[16,144,128]{2,1,0:T(8,128)(2,1)S(1)}, u32[]{:S(2)}, u32[]{:S(2)}) collective-permute-start(bf16[16,144,128]{2,1,0:T(8,128)(2,1)S(1)} %slice.8), channel_id=1, source_target_pairs={{0,4},{4,8},{8,12},{12,2},{2,14},{6,0},{10,6},{14,10},{1,5},{5,9},... | collective-permute-start | bytes 1769480 | tf_op jit(solution)/shard_map/ppermute | solution.py:456
  50.0 4.4 %collective-permute-start.1 = (bf16[16,144,128]{2,1,0:T(8,128)(2,1)S(1)}, bf16[16,144,128]{2,1,0:T(8,128)(2,1)S(1)}, u32[]{:S(2)}, u32[]{:S(2)}) collective-permute-start(bf16[16,144,128]{2,1,0:T(8,128)(2,1)S(1)} %slice.8), channel_id=1, source_target_pairs={{0,6},{4,10},{8,14},{12,0},{2,12},{6,2},{10,4},{14,8},{1,7},{5,11}... | collective-permute-start | bytes 1769480 | tf_op jit(solution)/shard_map/ppermute | solution.py:456
  54.4 2.1 collective-permute-start.12
  58.1 5.7 %collective-permute-start.2 = (bf16[16,72,128]{2,1,0:T(8,128)(2,1)S(1)}, bf16[16,72,128]{2,1,0:T(8,128)(2,1)S(1)}, u32[]{:S(2)}, u32[]{:S(2)}) collective-permute-start(bf16[16,72,128]{2,1,0:T(8,128)(2,1)S(1)} %slice.9), channel_id=1, source_target_pairs={{0,8},{4,12},{8,2},{12,6},{2,10},{6,14},{10,0},{14,4},{1,9},{5,13}... | collective-permute-start | bytes 884744 | tf_op jit(solution)/shard_map/ppermute | solution.py:456
  63.8 3.4 %collective-permute-start.3 = (bf16[16,72,128]{2,1,0:T(8,128)(2,1)S(1)}, bf16[16,72,128]{2,1,0:T(8,128)(2,1)S(1)}, u32[]{:S(2)}, u32[]{:S(2)}) collective-permute-start(bf16[16,72,128]{2,1,0:T(8,128)(2,1)S(1)} %slice.9), channel_id=1, source_target_pairs={{0,10},{4,14},{8,0},{12,4},{2,8},{6,12},{10,2},{14,6},{1,11},{5,15... | collective-permute-start | bytes 884744 | tf_op jit(solution)/shard_map/ppermute | solution.py:456
  67.2 38.8 %collective-permute-done.2.f1_ref = bf16[16,72,128]{2,1,0:T(8,128)(2,1)S(1)} collective-permute-done((bf16[16,72,128]{2,1,0:T(8,128)(2,1)S(1)}, bf16[16,72,128]{2,1,0:T(8,128)(2,1)S(1)}, u32[]{:S(2)}, u32[]{:S(2)}) %collective-permute-start.2) | collective-permute-done | bytes 294944 | tf_op jit(solution)/shard_map/ppermute | solution.py:456
  106.0 2.7 collective-permute-start.19
  112.4 2.7 collective-permute-start.22
  117.5 3.7 %rotate_grad.1.mine_ref = bf16[128,9216]{1,0:T(8,128)(2,1)S(1)} custom-call(bf16[16,360,128]{2,1,0:T(8,128)(2,1)S(1)} %copy-done.4, bf16[16,144,128]{2,1,0:T(8,128)(2,1)S(1)} %collective-permute-done.u1_ref, bf16[16,144,128]{2,1,0:T(8,128)(2,1)S(1)} %collective-permute-done.1.u2_ref, bf16[16,72,128]{2,1,0:T(8,128)(2,1)S(1)} %collective-permute-done.2.f1_ref, ...), custom_call_target="tpu_custom_call" | custom-call | flops 301989888 | bytes 5242880 | tf_op jit(solution)/shard_map/rotate_grad/pallas_call | solution.py:187
  121.3 1.7 collective-permute-start.4
  125.2 29.9 %collective-permute-done.11.a_ref = bf16[2,288,512]{2,1,0:T(8,128)(2,1)S(1)} collective-permute-done((bf16[2,288,512]{2,1,0:T(8,128)(2,1)S(1)}, bf16[2,288,512]{2,1,0:T(8,128)(2,1)S(1)}, u32[]{:S(2)}, u32[]{:S(2)}) %collective-permute-start.11) | collective-permute-done | bytes 589856 | tf_op jit(solution)/shard_map/ppermute | solution.py:435
  155.3 2.8 %collective-permute-start.20 = (bf16[4,288,512]{2,1,0:T(8,128)(2,1)S(1)}, bf16[4,288,512]{2,1,0:T(8,128)(2,1)}, u32[]{:S(2)}, u32[]{:S(2)}) collective-permute-start(bf16[4,288,512]{2,1,0:T(8,128)(2,1)S(1)} %join.7.q_ref), channel_id=1, source_target_pairs={{0,48},{16,0},{32,16},{48,32},{1,49},{17,1},{33,17},{49,33},{2,50}... | collective-permute-start | bytes 3538952 | tf_op jit(solution)/shard_map/ppermute | solution.py:435
  159.1 2.7 collective-permute-start.13
  162.8 18.8 %collective-permute-done.25.q_ref = bf16[4,288,512]{2,1,0:T(8,128)(2,1)S(1)} collective-permute-done((bf16[4,288,512]{2,1,0:T(8,128)(2,1)S(1)}, bf16[4,288,512]{2,1,0:T(8,128)(2,1)S(1)}, u32[]{:S(2)}, u32[]{:S(2)}) %collective-permute-start.25) | collective-permute-done | bytes 1179680 | tf_op jit(solution)/shard_map/ppermute | solution.py:435
  185.1 2.7 collective-permute-start.21
  194.8 4.0 %shard_map.89 = (f32[256,512]{1,0:T(8,128)S(1)}, f32[4,256,512]{2,1,0:T(8,128)S(1)}, bf16[1024,512]{1,0:T(8,128)(2,1)S(1)}) custom-call(s32[4]{0:T(128)S(1)} %copy-done.25, bf16[128,9216]{1,0:T(8,128)(2,1)S(1)} %rotate_grad.1.mine_ref, bf16[128,9216]{1,0:T(8,128)(2,1)S(1)} %copy-done.1, bf16[4,288,512]{2,1,0:T(8,128)(2,1)S(1)} %join.6.p_ref, ...), custom_call_target="tpu_custom_call" | custom-call | flops 1073741824 | bytes 6291456 | tf_op jit(solution)/shard_map/pallas_call | solution.py:329
  198.8 3.5 %shard_map.86 = (f32[256,512]{1,0:T(8,128)S(1)}, f32[1,256,512]{2,1,0:T(8,128)S(1)}, bf16[1024,512]{1,0:T(8,128)(2,1)S(1)}) custom-call(s32[4]{0:T(128)S(1)} %copy-done.25, bf16[128,9216]{1,0:T(8,128)(2,1)S(1)} %rotate_grad.1.mine_ref, bf16[128,9216]{1,0:T(8,128)(2,1)S(1)} %copy-done.1, bf16[4,288,512]{2,1,0:T(8,128)(2,1)S(1)} %copy-done.6, ...), custom_call_target="tpu_custom_call" | custom-call | flops 1073741824 | bytes 6291456 | tf_op jit(solution)/shard_map/pallas_call | solution.py:329
  202.4 4.5 %shard_map.87 = (f32[256,512]{1,0:T(8,128)S(1)}, f32[1,256,512]{2,1,0:T(8,128)S(1)}, bf16[1024,512]{1,0:T(8,128)(2,1)S(1)}) custom-call(s32[4]{0:T(128)S(1)} %copy-done.25, bf16[128,9216]{1,0:T(8,128)(2,1)S(1)} %rotate_grad.1.mine_ref, bf16[128,9216]{1,0:T(8,128)(2,1)S(1)} %copy-done.1, ...), custom_call_target="tpu_custom_call", output_to_operand_aliasing={{0}: (5, {}), {2}: (6, {})} | custom-call | flops 1073741824 | bytes 6291456 | tf_op jit(solution)/shard_map/pallas_call | solution.py:329
  206.9 4.1 %shard_map.88 = (f32[256,512]{1,0:T(8,128)S(1)}, f32[1,256,512]{2,1,0:T(8,128)S(1)}, bf16[1024,512]{1,0:T(8,128)(2,1)S(1)}) custom-call(s32[4]{0:T(128)S(1)} %copy-done.25, bf16[128,9216]{1,0:T(8,128)(2,1)S(1)} %rotate_grad.1.mine_ref, bf16[128,9216]{1,0:T(8,128)(2,1)S(1)} %copy-done.1, ...), custom_call_target="tpu_custom_call", output_to_operand_aliasing={{0}: (5, {}), {2}: (6, {})} | custom-call | flops 1073741824 | bytes 6291456 | tf_op jit(solution)/shard_map/pallas_call | solution.py:329
  211.1 3.0 %shard_map.90 = (f32[256,512]{1,0:T(8,128)S(1)}, f32[4,256,512]{2,1,0:T(8,128)S(1)}, bf16[1024,512]{1,0:T(8,128)(2,1)S(1)}) custom-call(s32[4]{0:T(128)S(1)} %copy-done.25, bf16[128,9216]{1,0:T(8,128)(2,1)S(1)} %rotate_grad.1.mine_ref, bf16[128,9216]{1,0:T(8,128)(2,1)S(1)} %copy-done.1, ...), custom_call_target="tpu_custom_call", output_to_operand_aliasing={{0}: (5, {}), {1}: (6, {}), {2}: (7, {})} | custom-call | flops 1073741824 | bytes 6291456 | tf_op jit(solution)/shard_map/pallas_call | solution.py:329
  214.1 5.0 %shard_map.91 = (f32[256,512]{1,0:T(8,128)S(1)}, f32[4,256,512]{2,1,0:T(8,128)S(1)}, bf16[1024,512]{1,0:T(8,128)(2,1)S(1)}) custom-call(s32[4]{0:T(128)S(1)} %copy-done.25, bf16[128,9216]{1,0:T(8,128)(2,1)S(1)} %rotate_grad.1.mine_ref, bf16[128,9216]{1,0:T(8,128)(2,1)S(1)} %copy-done.1, ...), custom_call_target="tpu_custom_call", output_to_operand_aliasing={{0}: (5, {}), {1}: (6, {}), {2}: (7, {})} | custom-call | flops 1073741824 | bytes 6291456 | tf_op jit(solution)/shard_map/pallas_call | solution.py:329
  219.1 13.4 %collective-permute-done.21.refs_3_ = bf16[4,288,512]{2,1,0:T(8,128)(2,1)} collective-permute-done((bf16[4,288,512]{2,1,0:T(8,128)(2,1)}, bf16[4,288,512]{2,1,0:T(8,128)(2,1)}, u32[]{:S(2)}, u32[]{:S(2)}) %collective-permute-start.21) | collective-permute-done | bytes 1179680 | tf_op jit(solution)/shard_map/ppermute | solution.py:435
  232.5 12.9 %last.1 = (f32[1024,256]{1,0:T(8,128)}, f32[4,1024]{1,0:T(4,128)S(1)}) custom-call(s32[4]{0:T(128)S(1)} %copy-done.25, f32[5]{0:T(128)S(1)} %pad_maximum_fusion.scale_ref, bf16[128,9216]{1,0:T(8,128)(2,1)S(1)} %rotate_grad.1.mine_ref, bf16[128,9216]{1,0:T(8,128)(2,1)S(1)} %copy-done.2, bf16[4,288,512]{2,1,0:T(8,128)(2,1)} %collective-permute-done.10.refs_0_, ...), custom_call_target="tpu_custom_call" | custom-call | tf_op jit(solution)/shard_map/last/pallas_call | solution.py:411
  245.8 24.6 %all_to_all.10 = f32[256,2,128]{2,1,0:T(2,128)S(1)} all-to-all(f32[256,2,128]{2,1,0:T(2,128)S(1)} %broadcast_in_dim.10), channel_id=1, replica_groups=mesh['dp_0'=4,'dp_1'=4,'dp_2'=4,'mp_0'=2,'mp_1'=2] {'dp_0','dp_1','dp_2'..., dimensions={0} | all-to-all | bytes 524288 | tf_op jit(solution)/shard_map/all_to_all | solution.py:495
  (102 shorter events, 26.2 us)
Async XLA Ops:
  6.3 37.0 %all-to-all-start = ((bf16[16,360,128]{2,1,0:T(8,128)(2,1)}), bf16[16,360,128]{2,1,0:T(8,128)(2,1)S(1)}, u32[]{:S(2)}, u32[]{:S(2)}) async-start(bf16[16,360,128]{2,1,0:T(8,128)(2,1)} %pack.1), calls=%async_computation | async-start | bytes 2949120 | tf_op jit(solution)/shard_map/all_to_all | solution.py:470
  14.0 10.9 %collective-permute-start.5 = (bf16[144,1024]{1,0:T(8,128)(2,1)S(1)}, bf16[144,1024]{1,0:T(8,128)(2,1)S(1)}, u32[]{:S(2)}, u32[]{:S(2)}) collective-permute-start(bf16[144,1024]{1,0:T(8,128)(2,1)S(1)} %copy-done.11), channel_id=1, source_target_pairs={{0,4},{4,8},{8,12},{12,0},{1,5},{5,9},{9,13},{13,1},{2,6},{6,10},{... | collective-permute-start | bytes 884744 | tf_op jit(solution)/shard_map/ppermute | solution.py:435
  15.7 22.9 %collective-permute-start.6 = (bf16[144,1024]{1,0:T(8,128)(2,1)S(1)}, bf16[144,1024]{1,0:T(8,128)(2,1)S(1)}, u32[]{:S(2)}, u32[]{:S(2)}) collective-permute-start(bf16[144,1024]{1,0:T(8,128)(2,1)S(1)} %copy-done.11), channel_id=1, source_target_pairs={{0,8},{4,12},{8,0},{12,4},{1,9},{5,13},{9,1},{13,5},{2,10},{6,14},... | collective-permute-start | bytes 884744 | tf_op jit(solution)/shard_map/ppermute | solution.py:435
  18.7 19.9 %collective-permute-start.7 = (bf16[144,1024]{1,0:T(8,128)(2,1)S(1)}, bf16[144,1024]{1,0:T(8,128)(2,1)S(1)}, u32[]{:S(2)}, u32[]{:S(2)}) collective-permute-start(bf16[144,1024]{1,0:T(8,128)(2,1)S(1)} %copy-done.11), channel_id=1, source_target_pairs={{0,12},{4,0},{8,4},{12,8},{1,13},{5,1},{9,5},{13,9},{2,14},{6,2},{... | collective-permute-start | bytes 884744 | tf_op jit(solution)/shard_map/ppermute | solution.py:435
  39.5 66.5 %copy-start.20 = (bf16[2,288,512]{2,1,0:T(8,128)(2,1)}, bf16[2,288,512]{2,1,0:T(8,128)(2,1)S(1)}, u32[]{:S(2)}) copy-start(bf16[2,288,512]{2,1,0:T(8,128)(2,1)S(1)} %get-tuple-element.25.a_ref) | copy-start | bytes 1769476
  39.5 14.9 %collective-permute-start.18 = (bf16[2,288,512]{2,1,0:T(8,128)(2,1)S(1)}, bf16[2,288,512]{2,1,0:T(8,128)(2,1)}, u32[]{:S(2)}, u32[]{:S(2)}) collective-permute-start(bf16[2,288,512]{2,1,0:T(8,128)(2,1)S(1)} %get-tuple-element.25.a_ref), channel_id=1, source_target_pairs={{0,192},{64,0},{128,64},{192,128},{1,193},{65,1},{129,65},{193,129... | collective-permute-start | bytes 1769480 | tf_op jit(solution)/shard_map/ppermute | solution.py:435
  42.1 15.2 %collective-permute-start.15 = (bf16[2,288,512]{2,1,0:T(8,128)(2,1)S(1)}, bf16[2,288,512]{2,1,0:T(8,128)(2,1)S(1)}, u32[]{:S(2)}, u32[]{:S(2)}) collective-permute-start(bf16[2,288,512]{2,1,0:T(8,128)(2,1)S(1)} %get-tuple-element.25.a_ref), channel_id=1, source_target_pairs={{0,64},{64,128},{128,192},{192,0},{1,65},{65,129},{129,193},{193,1... | collective-permute-start | bytes 1769480 | tf_op jit(solution)/shard_map/ppermute | solution.py:435
  42.1 21.7 %collective-permute-start.8 = (bf16[2,288,512]{2,1,0:T(8,128)(2,1)}, bf16[2,288,512]{2,1,0:T(8,128)(2,1)S(1)}, u32[]{:S(2)}, u32[]{:S(2)}) collective-permute-start(bf16[2,288,512]{2,1,0:T(8,128)(2,1)} %get-tuple-element.24.a_ref), channel_id=1, source_target_pairs={{0,16},{16,32},{32,48},{48,0},{1,17},{17,33},{33,49},{49,1},{2,18}... | collective-permute-start | bytes 1769480 | tf_op jit(solution)/shard_map/ppermute | solution.py:435
  43.3 67.8 %copy-start.3 = (bf16[16,360,128]{2,1,0:T(8,128)(2,1)}, bf16[16,360,128]{2,1,0:T(8,128)(2,1)S(1)}, u32[]{:S(2)}) copy-start(bf16[16,360,128]{2,1,0:T(8,128)(2,1)S(1)} %all-to-all-done.own_ref) | copy-start | bytes 4423684
  43.3 69.0 %collective-permute-start = (bf16[16,144,128]{2,1,0:T(8,128)(2,1)S(1)}, bf16[16,144,128]{2,1,0:T(8,128)(2,1)S(1)}, u32[]{:S(2)}, u32[]{:S(2)}) collective-permute-start(bf16[16,144,128]{2,1,0:T(8,128)(2,1)S(1)} %slice.8), channel_id=1, source_target_pairs={{0,4},{4,8},{8,12},{12,2},{2,14},{6,0},{10,6},{14,10},{1,5},{5,9},... | collective-permute-start | bytes 1769480 | tf_op jit(solution)/shard_map/ppermute | solution.py:456
  50.0 65.0 %collective-permute-start.1 = (bf16[16,144,128]{2,1,0:T(8,128)(2,1)S(1)}, bf16[16,144,128]{2,1,0:T(8,128)(2,1)S(1)}, u32[]{:S(2)}, u32[]{:S(2)}) collective-permute-start(bf16[16,144,128]{2,1,0:T(8,128)(2,1)S(1)} %slice.8), channel_id=1, source_target_pairs={{0,6},{4,10},{8,14},{12,0},{2,12},{6,2},{10,4},{14,8},{1,7},{5,11}... | collective-permute-start | bytes 1769480 | tf_op jit(solution)/shard_map/ppermute | solution.py:456
  54.4 66.8 %collective-permute-start.12 = (bf16[2,288,512]{2,1,0:T(8,128)(2,1)}, bf16[2,288,512]{2,1,0:T(8,128)(2,1)S(1)}, u32[]{:S(2)}, u32[]{:S(2)}) collective-permute-start(bf16[2,288,512]{2,1,0:T(8,128)(2,1)} %get-tuple-element.24.a_ref), channel_id=1, source_target_pairs={{0,48},{16,0},{32,16},{48,32},{1,49},{17,1},{33,17},{49,33},{2,50}... | collective-permute-start | bytes 1769480 | tf_op jit(solution)/shard_map/ppermute | solution.py:435
  58.1 47.9 %collective-permute-start.2 = (bf16[16,72,128]{2,1,0:T(8,128)(2,1)S(1)}, bf16[16,72,128]{2,1,0:T(8,128)(2,1)S(1)}, u32[]{:S(2)}, u32[]{:S(2)}) collective-permute-start(bf16[16,72,128]{2,1,0:T(8,128)(2,1)S(1)} %slice.9), channel_id=1, source_target_pairs={{0,8},{4,12},{8,2},{12,6},{2,10},{6,14},{10,0},{14,4},{1,9},{5,13}... | collective-permute-start | bytes 884744 | tf_op jit(solution)/shard_map/ppermute | solution.py:456
  63.8 48.4 %copy-start.18 = (bf16[2,288,512]{2,1,0:T(8,128)(2,1)}, bf16[2,288,512]{2,1,0:T(8,128)(2,1)S(1)}, u32[]{:S(2)}) copy-start(bf16[2,288,512]{2,1,0:T(8,128)(2,1)S(1)} %collective-permute-done.8.b_ref) | copy-start | bytes 1769476
  63.8 48.5 %collective-permute-start.3 = (bf16[16,72,128]{2,1,0:T(8,128)(2,1)S(1)}, bf16[16,72,128]{2,1,0:T(8,128)(2,1)S(1)}, u32[]{:S(2)}, u32[]{:S(2)}) collective-permute-start(bf16[16,72,128]{2,1,0:T(8,128)(2,1)S(1)} %slice.9), channel_id=1, source_target_pairs={{0,10},{4,14},{8,0},{12,4},{2,8},{6,12},{10,2},{14,6},{1,11},{5,15... | collective-permute-start | bytes 884744 | tf_op jit(solution)/shard_map/ppermute | solution.py:456
  106.0 17.0 %collective-permute-start.19 = (bf16[2,288,512]{2,1,0:T(8,128)(2,1)}, bf16[2,288,512]{2,1,0:T(8,128)(2,1)S(1)}, u32[]{:S(2)}, u32[]{:S(2)}) collective-permute-start(bf16[2,288,512]{2,1,0:T(8,128)(2,1)} %collective-permute-done.18.b_ref), channel_id=1, source_target_pairs={{0,192},{64,0},{128,64},{192,128},{1,193},{65,1},{129,65},{193,129... | collective-permute-start | bytes 1769480 | tf_op jit(solution)/shard_map/ppermute | solution.py:435
  112.3 45.8 %collective-permute-start.9 = (bf16[4,288,512]{2,1,0:T(8,128)(2,1)S(1)}, bf16[4,288,512]{2,1,0:T(8,128)(2,1)}, u32[]{:S(2)}, u32[]{:S(2)}) collective-permute-start(bf16[4,288,512]{2,1,0:T(8,128)(2,1)S(1)} %join.4.p_ref), channel_id=1, source_target_pairs={{0,64},{64,128},{128,192},{192,0},{1,65},{65,129},{129,193},{193,1... | collective-permute-start | bytes 3538952 | tf_op jit(solution)/shard_map/ppermute | solution.py:435
  112.4 45.7 %collective-permute-start.22 = (bf16[4,288,512]{2,1,0:T(8,128)(2,1)S(1)}, bf16[4,288,512]{2,1,0:T(8,128)(2,1)S(1)}, u32[]{:S(2)}, u32[]{:S(2)}) collective-permute-start(bf16[4,288,512]{2,1,0:T(8,128)(2,1)S(1)} %join.4.p_ref), channel_id=1, source_target_pairs={{0,192},{64,0},{128,64},{192,128},{1,193},{65,1},{129,65},{193,129... | collective-permute-start | bytes 3538952 | tf_op jit(solution)/shard_map/ppermute | solution.py:435
  115.0 40.3 %collective-permute-start.16 = (bf16[4,288,512]{2,1,0:T(8,128)(2,1)S(1)}, bf16[4,288,512]{2,1,0:T(8,128)(2,1)}, u32[]{:S(2)}, u32[]{:S(2)}) collective-permute-start(bf16[4,288,512]{2,1,0:T(8,128)(2,1)S(1)} %join.6.p_ref), channel_id=1, source_target_pairs={{0,16},{16,32},{32,48},{48,0},{1,17},{17,33},{33,49},{49,1},{2,18}... | collective-permute-start | bytes 3538952 | tf_op jit(solution)/shard_map/ppermute | solution.py:435
  121.3 66.5 %collective-permute-start.4 = (bf16[128,9216]{1,0:T(8,128)(2,1)S(1)}, bf16[128,9216]{1,0:T(8,128)(2,1)S(1)}, u32[]{:S(2)}, u32[]{:S(2)}) collective-permute-start(bf16[128,9216]{1,0:T(8,128)(2,1)S(1)} %rotate_grad.1.mine_ref), channel_id=1, source_target_pairs={{0,1},{1,0},{2,3},{3,2},{4,5},{5,4},{6,7},{7,6},{8,9},{9,8},{10,11... | collective-permute-start | bytes 7077896 | tf_op jit(solution)/shard_map/ppermute | solution.py:474
  123.0 32.0 %collective-permute-start.11 = (bf16[2,288,512]{2,1,0:T(8,128)(2,1)S(1)}, bf16[2,288,512]{2,1,0:T(8,128)(2,1)S(1)}, u32[]{:S(2)}, u32[]{:S(2)}) collective-permute-start(bf16[2,288,512]{2,1,0:T(8,128)(2,1)S(1)} %copy-done.19), channel_id=1, source_target_pairs={{0,16},{16,32},{32,48},{48,0},{1,17},{17,33},{33,49},{49,1},{2,18}... | collective-permute-start | bytes 1769480 | tf_op jit(solution)/shard_map/ppermute | solution.py:435
  125.2 62.6 %copy-start.7 = (bf16[4,288,512]{2,1,0:T(8,128)(2,1)}, bf16[4,288,512]{2,1,0:T(8,128)(2,1)S(1)}, u32[]{:S(2)}) copy-start(bf16[4,288,512]{2,1,0:T(8,128)(2,1)S(1)} %join.7.q_ref) | copy-start | bytes 3538948
  125.2 65.3 %copy-start.25 = (s32[4]{0:T(128)S(1)}, s32[4]{0:T(128)}, u32[]{:S(2)}) copy-start(s32[4]{0:T(128)} %len_ref.15) | copy-start | bytes 52
  155.1 26.5 %collective-permute-start.25 = (bf16[4,288,512]{2,1,0:T(8,128)(2,1)S(1)}, bf16[4,288,512]{2,1,0:T(8,128)(2,1)S(1)}, u32[]{:S(2)}, u32[]{:S(2)}) collective-permute-start(bf16[4,288,512]{2,1,0:T(8,128)(2,1)S(1)} %join.7.q_ref), channel_id=1, source_target_pairs={{0,16},{16,32},{32,48},{48,0},{1,17},{17,33},{33,49},{49,1},{2,18}... | collective-permute-start | bytes 3538952 | tf_op jit(solution)/shard_map/ppermute | solution.py:435
  155.3 27.3 %collective-permute-start.20 = (bf16[4,288,512]{2,1,0:T(8,128)(2,1)S(1)}, bf16[4,288,512]{2,1,0:T(8,128)(2,1)}, u32[]{:S(2)}, u32[]{:S(2)}) collective-permute-start(bf16[4,288,512]{2,1,0:T(8,128)(2,1)S(1)} %join.7.q_ref), channel_id=1, source_target_pairs={{0,48},{16,0},{32,16},{48,32},{1,49},{17,1},{33,17},{49,33},{2,50}... | collective-permute-start | bytes 3538952 | tf_op jit(solution)/shard_map/ppermute | solution.py:435
  158.1 26.0 %collective-permute-start.23 = (bf16[4,288,512]{2,1,0:T(8,128)(2,1)S(1)}, bf16[4,288,512]{2,1,0:T(8,128)(2,1)S(1)}, u32[]{:S(2)}, u32[]{:S(2)}) collective-permute-start(bf16[4,288,512]{2,1,0:T(8,128)(2,1)S(1)} %join.5.q_ref), channel_id=1, source_target_pairs={{0,64},{64,128},{128,192},{192,0},{1,65},{65,129},{129,193},{193,1... | collective-permute-start | bytes 3538952 | tf_op jit(solution)/shard_map/ppermute | solution.py:435
  159.1 26.0 %collective-permute-start.13 = (bf16[4,288,512]{2,1,0:T(8,128)(2,1)S(1)}, bf16[4,288,512]{2,1,0:T(8,128)(2,1)}, u32[]{:S(2)}, u32[]{:S(2)}) collective-permute-start(bf16[4,288,512]{2,1,0:T(8,128)(2,1)S(1)} %join.5.q_ref), channel_id=1, source_target_pairs={{0,192},{64,0},{128,64},{192,128},{1,193},{65,1},{129,65},{193,129... | collective-permute-start | bytes 3538952 | tf_op jit(solution)/shard_map/ppermute | solution.py:435
  182.6 31.4 %collective-permute-start.24 = (bf16[4,288,512]{2,1,0:T(8,128)(2,1)S(1)}, bf16[4,288,512]{2,1,0:T(8,128)(2,1)}, u32[]{:S(2)}, u32[]{:S(2)}) collective-permute-start(bf16[4,288,512]{2,1,0:T(8,128)(2,1)S(1)} %join.6.p_ref), channel_id=1, source_target_pairs={{0,48},{16,0},{32,16},{48,32},{1,49},{17,1},{33,17},{49,33},{2,50}... | collective-permute-start | bytes 3538952 | tf_op jit(solution)/shard_map/ppermute | solution.py:435
  182.6 36.5 %collective-permute-start.10 = (bf16[4,288,512]{2,1,0:T(8,128)(2,1)}, bf16[4,288,512]{2,1,0:T(8,128)(2,1)}, u32[]{:S(2)}, u32[]{:S(2)}) collective-permute-start(bf16[4,288,512]{2,1,0:T(8,128)(2,1)} %collective-permute-done.9.p_ref), channel_id=1, source_target_pairs={{0,64},{64,128},{128,192},{192,0},{1,65},{65,129},{129,193},{193,1... | collective-permute-start | bytes 3538952 | tf_op jit(solution)/shard_map/ppermute | solution.py:435
  185.1 34.0 %collective-permute-start.17 = (bf16[4,288,512]{2,1,0:T(8,128)(2,1)}, bf16[4,288,512]{2,1,0:T(8,128)(2,1)}, u32[]{:S(2)}, u32[]{:S(2)}) collective-permute-start(bf16[4,288,512]{2,1,0:T(8,128)(2,1)} %collective-permute-done.16.p_ref), channel_id=1, source_target_pairs={{0,16},{16,32},{32,48},{48,0},{1,17},{17,33},{33,49},{49,1},{2,18}... | collective-permute-start | bytes 3538952 | tf_op jit(solution)/shard_map/ppermute | solution.py:435
  185.1 47.4 %collective-permute-start.21 = (bf16[4,288,512]{2,1,0:T(8,128)(2,1)}, bf16[4,288,512]{2,1,0:T(8,128)(2,1)}, u32[]{:S(2)}, u32[]{:S(2)}) collective-permute-start(bf16[4,288,512]{2,1,0:T(8,128)(2,1)} %collective-permute-done.20.q_ref), channel_id=1, source_target_pairs={{0,48},{16,0},{32,16},{48,32},{1,49},{17,1},{33,17},{49,33},{2,50}... | collective-permute-start | bytes 3538952 | tf_op jit(solution)/shard_map/ppermute | solution.py:435
  189.2 43.3 %collective-permute-start.14 = (bf16[4,288,512]{2,1,0:T(8,128)(2,1)}, bf16[4,288,512]{2,1,0:T(8,128)(2,1)}, u32[]{:S(2)}, u32[]{:S(2)}) collective-permute-start(bf16[4,288,512]{2,1,0:T(8,128)(2,1)} %collective-permute-done.13.q_ref), channel_id=1, source_target_pairs={{0,192},{64,0},{128,64},{192,128},{1,193},{65,1},{129,65},{193,129... | collective-permute-start | bytes 3538952 | tf_op jit(solution)/shard_map/ppermute | solution.py:435
  (21 other events, 78.8 us)
where the time goes:
time: 272 us; the launch traced here: 271 us
  waiting for transfers between devices  122 us (45%)
  starting transfers between devices  57.8 us (21%)
  Pallas kernels  50.2 us (18%)
  blocking collectives  24.6 us (9%)
  local copies, waits for them, and re-layouts  13.8 us (5%)
    ppermute x21, waiting for transfers between devices, shift(): return lax.ppermute(x, axis, [(i, (i + step) % RING) for i in range(RING)])  83.4 us
    ppermute x4, waiting for transfers between devices, along_z(): return lax.ppermute(x, (Z, H), [(at_z(a), at_z(b)) for a, b in pairs])  38.8 us
    ppermute x21, starting transfers between devices, shift(): return lax.ppermute(x, axis, [(i, (i + step) % RING) for i in range(RING)])  28.2 us
    all_to_all x1, blocking collectives, local(): scores = lax.all_to_all(everywhere, ALL, 0, 0, tiled=True).sum(0)  24.6 us
    pallas_call x6, Pallas kernels, group(): pl.pallas_call(functools.partial(group_kernel, part, outer), out_shape=(j...  24.2 us
    ppermute x4, starting transfers between devices, along_z(): return lax.ppermute(x, (Z, H), [(at_z(a), at_z(b)) for a, b in pairs])  20.2 us
    pallas_call x1, Pallas kernels, last(): pl.pallas_call(last_kernel, out_shape=(jax.ShapeDtypeStruct((FEAT, COLS),...  12.9 us
    unnamed x52, local copies, waits for them, and re-layouts  12.8 us
  transfers between devices with their start and end apart: 27, of which 8 were waited for; matrix products, arithmetic and copies ran while one was open for 0% of the time, Pallas kernels for 12%

commit v1 on v0

--- a/solution.py
+++ b/solution.py
@@ -229,27 +229,29 @@
     )(*blocks)
 
 
-def join_kernel(a_ref, b_ref, out_ref, sem):
-    copies = [
-        pltpu.make_async_copy(ref, out_ref.at[pl.ds(2 * n, 2)], sem.at[n])
-        for n, ref in enumerate((a_ref, b_ref))
-    ]
+def join_kernel(*refs):
+    ins, out_ref, sem = refs[:-2], refs[-2], refs[-1]
+    copies, at = [], 0
+    for n, ref in enumerate(ins):
+        size = ref.shape[0]
+        copies.append(pltpu.make_async_copy(ref, out_ref.at[pl.ds(at, size)], sem.at[n]))
+        at += size
     for c in copies:
         c.start()
     for c in copies:
         c.wait()
 
 
-def join(a, b):
+def join(*pieces):
     return pl.pallas_call(
         join_kernel,
         out_shape=jax.ShapeDtypeStruct((4, 2 * ROWS, HALF), jnp.bfloat16),
-        in_specs=[spec(ANY)] * 2,
+        in_specs=[spec(ANY)] * len(pieces),
         out_specs=spec(VM),
-        scratch_shapes=[pltpu.SemaphoreType.DMA((2,))],
+        scratch_shapes=[pltpu.SemaphoreType.DMA((len(pieces),))],
         compiler_params=pltpu.CompilerParams(vmem_limit_bytes=4 << 20),
         name="join",
-    )(a, b)
+    )(*pieces)
 
 
 def place(at, slot):
@@ -279,10 +281,10 @@
 SEMS = 2 + 2 * RING
 
 
-def contract(part, outer, len_ref, u_ref, g_ref, mom_ref, seq_ref, q_ref):
+def contract(part, outer, pair, len_ref, u_ref, g_ref, mom_ref, seq_ref, q_ref):
     y, x, _, _, _ = where()
 
-    @pl.loop(0, HALVES)
+    @pl.loop(pair * RING, (pair + 1) * RING)
     def _(n):
         v = place(x if part == 0 else y, n // 2)
         half = lax.rem(n, 2)
@@ -305,19 +307,21 @@
     refs = refs[carried:]
     mom_ref, seq_ref, qout_ref, u_ref, g_ref, sem = refs
     copies = group_copies(part, outer, (p_ref, q_ref), (mine_ref, other_ref), u_ref, g_ref, sem)
-    for c in copies:
+    for c in (*copies[2:], *copies[:2]):
         c.start()
     if not outer:
         mom_ref[...] = jnp.zeros_like(mom_ref)
     if not (outer and part):
         seq_ref[...] = jnp.zeros_like(seq_ref)
-    for c in copies:
-        c.wait()
     if part == 0:
         y = lax.axis_index(Y)
         row = pl.multiple_of(place(y, outer) * 256, 256)
         qout_ref = qout_ref.at[pl.ds(row, 256), :]
-    contract(part, outer, len_ref, u_ref, g_ref, mom_ref, seq_ref, qout_ref)
+    for c in copies[2:]:
+        c.wait()
+    for pair in range(2):
+        copies[pair].wait()
+        contract(part, outer, pair, len_ref, u_ref, g_ref, mom_ref, seq_ref, qout_ref)
 
 
 def group(part, outer, lengths, mine, other, pairs, mom, seqs, queries):
@@ -358,13 +362,14 @@
     moms, seq_a, seq_b, q_ins, refs = refs[0:2], refs[2:5], refs[5], refs[6:8], refs[8:]
     out_ref, score_ref, w_ref, s_ref, q_ref, u_ref, g_ref, qg_ref, p_ref, sem = refs
     y, _, _, _, c = where()
-    copies = []
-    for part in range(2):
-        copies += group_copies(part, FAR, pairs[part], (mine_ref, other_ref), u_ref.at[part], g_ref.at[part], sem.at[part])
-    for m, ref in enumerate((mine_ref, other_ref)):
-        copies.append(pltpu.make_async_copy(ref.at[:, pl.ds(TOKENS, QROWS)], qg_ref.at[m], sem.at[2, m]))
-    for copy in copies:
-        copy.start()
+    copies = [
+        group_copies(part, FAR, pairs[part], (mine_ref, other_ref), u_ref.at[part], g_ref.at[part], sem.at[part])
+        for part in range(2)
+    ]
+    copies.append([pltpu.make_async_copy(ref.at[:, pl.ds(TOKENS, QROWS)], qg_ref.at[m], sem.at[2, m]) for m, ref in enumerate((mine_ref, other_ref))])
+    for some in copies:
+        for copy in (*some[2:], *some[:2]):
+            copy.start()
     for part in range(2):
         w_ref[part] = moms[part][...]
         q_ref[part] = q_ins[part][...]
@@ -373,11 +378,17 @@
     far = place(y, FAR)
     s_ref[0, far] = jnp.zeros((COLS, HALF), jnp.float32)
     s_ref[1] = seq_b[...]
-    for copy in copies:
+    row = pl.multiple_of(far * 256, 256)
+    seq_refs = s_ref.at[0, pl.ds(far, 1)], s_ref.at[1]
+    q_refs = q_ref.at[0, pl.ds(row, 256), :], q_ref.at[1]
+    for part in range(2):
+        for copy in copies[part][2:]:
+            copy.wait()
+        for pair in range(2):
+            copies[part][pair].wait()
+            contract(part, FAR, pair, len_ref, u_ref.at[part], g_ref.at[part], w_ref.at[part], seq_refs[part], q_refs[part])
+    for copy in copies[2]:
         copy.wait()
-    row = pl.multiple_of(far * 256, 256)
-    contract(0, FAR, len_ref, u_ref.at[0], g_ref.at[0], w_ref.at[0], s_ref.at[0, pl.ds(far, 1)], q_ref.at[0, pl.ds(row, 256), :])
-    contract(1, FAR, len_ref, u_ref.at[1], g_ref.at[1], w_ref.at[1], s_ref.at[1], q_ref.at[1])
 
     mine_at = pl.multiple_of(c * BLOCK, BLOCK)
     other_at = pl.multiple_of((1 - c) * BLOCK, BLOCK)
@@ -491,8 +502,9 @@
     moments, per_row = last(seq_lengths, scales, mine, other, far, carried)
     per_query = jnp.sum(per_row.reshape(SEQS, QUERIES, QUERY_LEN), axis=2)
     partial = per_query.reshape(2, 128) / math.sqrt(QUERY_LEN * D * FF)
-    everywhere = jnp.broadcast_to(partial[None], (256, 2, 128))
-    scores = lax.all_to_all(everywhere, ALL, 0, 0, tiled=True).sum(0)
+    partial += lax.ppermute(partial, C, [(0, 1), (1, 0)])
+    everywhere = jnp.broadcast_to(partial[None], (128, 2, 128))
+    scores = lax.all_to_all(everywhere, (Y, X, Z, H), 0, 0, tiled=True).sum(0)
     return moments, scores.reshape(SEQS, QUERIES).T
 
 

time: 272 us -> 268 us (0.985)
  blocking collectives: 24.6 us -> 17.2 us
  starting transfers between devices: 57.8 us -> 61.7 us
    all_to_all x1, blocking collectives: 24.6 us -> 17.2 us  [local(): scores = lax.all_to_all(everywhere, (Y, X, Z, H), 0, 0, tiled=True).sum(0)]
    ppermute x0 -> x1, starting transfers between devices: none -> 3.93 us  [local(): partial += lax.ppermute(partial, C, [(0, 1), (1, 0)])]
  transfers between devices with their start and end apart: 27 -> 28, of which waited for: 8 -> 9; matrix products, arithmetic and copies ran while one was open for 0% -> 0% of each run, Pallas kernels for 12% -> 12%
where the time goes in v1:
time: 268 us
  waiting for transfers between devices  124 us (46%)
  starting transfers between devices  61.7 us (23%)
  Pallas kernels  48.4 us (18%)
  blocking collectives  17.2 us (6%)
  local copies, waits for them, and re-layouts  13.7 us (5%)
    ppermute x21, waiting for transfers between devices, shift(): return lax.ppermute(x, axis, [(i, (i + step) % RING) for i in range(RING)])  84.1 us
    ppermute x4, waiting for transfers between devices, along_z(): return lax.ppermute(x, (Z, H), [(at_z(a), at_z(b)) for a, b in pairs])  38.8 us
    ppermute x21, starting transfers between devices, shift(): return lax.ppermute(x, axis, [(i, (i + step) % RING) for i in range(RING)])  28.1 us
    pallas_call x6, Pallas kernels, group(): pl.pallas_call(functools.partial(group_kernel, part, outer), out_shape=(j...  23.4 us
    ppermute x4, starting transfers between devices, along_z(): return lax.ppermute(x, (Z, H), [(at_z(a), at_z(b)) for a, b in pairs])  20.2 us
    all_to_all x1, blocking collectives, local(): scores = lax.all_to_all(everywhere, (Y, X, Z, H), 0, 0, tiled=True).sum(0)  17.2 us
    unnamed x52, local copies, waits for them, and re-layouts  12.8 us
    pallas_call x1, Pallas kernels, last(): pl.pallas_call(last_kernel, out_shape=(jax.ShapeDtypeStruct((FEAT, COLS),...  11.9 us
  transfers between devices with their start and end apart: 28, of which 9 were waited for; matrix products, arithmetic and copies ran while one was open for 0% of the time, Pallas kernels for 12%

profile of v1, /device:TPU:1, one launch (start us, length us, event | category | flops | bytes accessed | tf_op | source)
XLA Modules:
  0.0 267.5 jit_solution(16931603632300360554)
XLA Ops:
  0.6 2.0 rotate_act.1.after_ref.refs_0_
  2.7 3.6 %pack.1 = bf16[16,360,128]{2,1,0:T(8,128)(2,1)} custom-call(bf16[128,16384]{1,0:T(8,128)(2,1)} %g_ref.1, bf16[16,16384]{1,0:T(8,128)(2,1)} %q_ref.3, bf16[144,1024]{1,0:T(8,128)(2,1)} %rotate_act.1.after_ref.refs_0_), custom_call_target="tpu_custom_call" | custom-call | tf_op jit(solution)/shard_map/pack/pallas_call | solution.py:138
  6.2 7.7 %all-to-all-start = ((bf16[16,360,128]{2,1,0:T(8,128)(2,1)}), bf16[16,360,128]{2,1,0:T(8,128)(2,1)S(1)}, u32[]{:S(2)}, u32[]{:S(2)}) async-start(bf16[16,360,128]{2,1,0:T(8,128)(2,1)} %pack.1), calls=%async_computation | async-start | bytes 2949120 | tf_op jit(solution)/shard_map/all_to_all | solution.py:481
  15.7 3.0 %collective-permute-start.6 = (bf16[144,1024]{1,0:T(8,128)(2,1)S(1)}, bf16[144,1024]{1,0:T(8,128)(2,1)S(1)}, u32[]{:S(2)}, u32[]{:S(2)}) collective-permute-start(bf16[144,1024]{1,0:T(8,128)(2,1)S(1)} %copy-done.11), channel_id=1, source_target_pairs={{0,8},{4,12},{8,0},{12,4},{1,9},{5,13},{9,1},{13,5},{2,10},{6,14},... | collective-permute-start | bytes 884744 | tf_op jit(solution)/shard_map/ppermute | solution.py:446
  19.4 5.5 %collective-permute-done.5.refs_1_ = bf16[144,1024]{1,0:T(8,128)(2,1)S(1)} collective-permute-done((bf16[144,1024]{1,0:T(8,128)(2,1)S(1)}, bf16[144,1024]{1,0:T(8,128)(2,1)S(1)}, u32[]{:S(2)}, u32[]{:S(2)}) %collective-permute-start.5) | collective-permute-done | bytes 294944 | tf_op jit(solution)/shard_map/ppermute | solution.py:446
  24.9 13.6 %collective-permute-done.6.refs_2_ = bf16[144,1024]{1,0:T(8,128)(2,1)S(1)} collective-permute-done((bf16[144,1024]{1,0:T(8,128)(2,1)S(1)}, bf16[144,1024]{1,0:T(8,128)(2,1)S(1)}, u32[]{:S(2)}, u32[]{:S(2)}) %collective-permute-start.6) | collective-permute-done | bytes 294944 | tf_op jit(solution)/shard_map/ppermute | solution.py:446
  39.5 2.6 collective-permute-start.18
  43.3 6.7 %collective-permute-start = (bf16[16,144,128]{2,1,0:T(8,128)(2,1)S(1)}, bf16[16,144,128]{2,1,0:T(8,128)(2,1)S(1)}, u32[]{:S(2)}, u32[]{:S(2)}) collective-permute-start(bf16[16,144,128]{2,1,0:T(8,128)(2,1)S(1)} %slice.8), channel_id=1, source_target_pairs={{0,4},{4,8},{8,12},{12,2},{2,14},{6,0},{10,6},{14,10},{1,5},{5,9},... | collective-permute-start | bytes 1769480 | tf_op jit(solution)/shard_map/ppermute | solution.py:467
  50.0 4.4 %collective-permute-start.1 = (bf16[16,144,128]{2,1,0:T(8,128)(2,1)S(1)}, bf16[16,144,128]{2,1,0:T(8,128)(2,1)S(1)}, u32[]{:S(2)}, u32[]{:S(2)}) collective-permute-start(bf16[16,144,128]{2,1,0:T(8,128)(2,1)S(1)} %slice.8), channel_id=1, source_target_pairs={{0,6},{4,10},{8,14},{12,0},{2,12},{6,2},{10,4},{14,8},{1,7},{5,11}... | collective-permute-start | bytes 1769480 | tf_op jit(solution)/shard_map/ppermute | solution.py:467
  54.4 2.1 collective-permute-start.12
  58.1 5.7 %collective-permute-start.2 = (bf16[16,72,128]{2,1,0:T(8,128)(2,1)S(1)}, bf16[16,72,128]{2,1,0:T(8,128)(2,1)S(1)}, u32[]{:S(2)}, u32[]{:S(2)}) collective-permute-start(bf16[16,72,128]{2,1,0:T(8,128)(2,1)S(1)} %slice.9), channel_id=1, source_target_pairs={{0,8},{4,12},{8,2},{12,6},{2,10},{6,14},{10,0},{14,4},{1,9},{5,13}... | collective-permute-start | bytes 884744 | tf_op jit(solution)/shard_map/ppermute | solution.py:467
  63.8 3.4 %collective-permute-start.3 = (bf16[16,72,128]{2,1,0:T(8,128)(2,1)S(1)}, bf16[16,72,128]{2,1,0:T(8,128)(2,1)S(1)}, u32[]{:S(2)}, u32[]{:S(2)}) collective-permute-start(bf16[16,72,128]{2,1,0:T(8,128)(2,1)S(1)} %slice.9), channel_id=1, source_target_pairs={{0,10},{4,14},{8,0},{12,4},{2,8},{6,12},{10,2},{14,6},{1,11},{5,15... | collective-permute-start | bytes 884744 | tf_op jit(solution)/shard_map/ppermute | solution.py:467
  67.2 38.8 %collective-permute-done.2.f1_ref = bf16[16,72,128]{2,1,0:T(8,128)(2,1)S(1)} collective-permute-done((bf16[16,72,128]{2,1,0:T(8,128)(2,1)S(1)}, bf16[16,72,128]{2,1,0:T(8,128)(2,1)S(1)}, u32[]{:S(2)}, u32[]{:S(2)}) %collective-permute-start.2) | collective-permute-done | bytes 294944 | tf_op jit(solution)/shard_map/ppermute | solution.py:467
  106.0 2.7 collective-permute-start.19
  112.4 2.7 collective-permute-start.22
  117.5 3.7 %rotate_grad.1.mine_ref = bf16[128,9216]{1,0:T(8,128)(2,1)S(1)} custom-call(bf16[16,360,128]{2,1,0:T(8,128)(2,1)S(1)} %copy-done.4, bf16[16,144,128]{2,1,0:T(8,128)(2,1)S(1)} %collective-permute-done.u1_ref, bf16[16,144,128]{2,1,0:T(8,128)(2,1)S(1)} %collective-permute-done.1.u2_ref, bf16[16,72,128]{2,1,0:T(8,128)(2,1)S(1)} %collective-permute-done.2.f1_ref, ...), custom_call_target="tpu_custom_call" | custom-call | flops 301989888 | bytes 5242880 | tf_op jit(solution)/shard_map/rotate_grad/pallas_call | solution.py:187
  121.3 1.7 collective-permute-start.4
  125.2 29.9 %collective-permute-done.11.refs_0_ = bf16[2,288,512]{2,1,0:T(8,128)(2,1)S(1)} collective-permute-done((bf16[2,288,512]{2,1,0:T(8,128)(2,1)S(1)}, bf16[2,288,512]{2,1,0:T(8,128)(2,1)S(1)}, u32[]{:S(2)}, u32[]{:S(2)}) %collective-permute-start.11) | collective-permute-done | bytes 589856 | tf_op jit(solution)/shard_map/ppermute | solution.py:446
  155.3 2.8 %collective-permute-start.20 = (bf16[4,288,512]{2,1,0:T(8,128)(2,1)S(1)}, bf16[4,288,512]{2,1,0:T(8,128)(2,1)}, u32[]{:S(2)}, u32[]{:S(2)}) collective-permute-start(bf16[4,288,512]{2,1,0:T(8,128)(2,1)S(1)} %join.7.q_ref), channel_id=1, source_target_pairs={{0,48},{16,0},{32,16},{48,32},{1,49},{17,1},{33,17},{49,33},{2,50}... | collective-permute-start | bytes 3538952 | tf_op jit(solution)/shard_map/ppermute | solution.py:446
  159.1 2.7 collective-permute-start.13
  162.8 18.8 %collective-permute-done.25.q_ref = bf16[4,288,512]{2,1,0:T(8,128)(2,1)S(1)} collective-permute-done((bf16[4,288,512]{2,1,0:T(8,128)(2,1)S(1)}, bf16[4,288,512]{2,1,0:T(8,128)(2,1)S(1)}, u32[]{:S(2)}, u32[]{:S(2)}) %collective-permute-start.25) | collective-permute-done | bytes 1179680 | tf_op jit(solution)/shard_map/ppermute | solution.py:446
  185.1 2.7 collective-permute-start.21
  194.7 4.0 %shard_map.89 = (f32[256,512]{1,0:T(8,128)S(1)}, f32[4,256,512]{2,1,0:T(8,128)S(1)}, bf16[1024,512]{1,0:T(8,128)(2,1)S(1)}) custom-call(s32[4]{0:T(128)S(1)} %copy-done.25, bf16[128,9216]{1,0:T(8,128)(2,1)S(1)} %rotate_grad.1.mine_ref, bf16[128,9216]{1,0:T(8,128)(2,1)S(1)} %copy-done.1, bf16[4,288,512]{2,1,0:T(8,128)(2,1)S(1)} %join.6.p_ref, ...), custom_call_target="tpu_custom_call" | custom-call | flops 1073741824 | bytes 6291456 | tf_op jit(solution)/shard_map/pallas_call | solution.py:333
  198.8 3.5 %shard_map.86 = (f32[256,512]{1,0:T(8,128)S(1)}, f32[1,256,512]{2,1,0:T(8,128)S(1)}, bf16[1024,512]{1,0:T(8,128)(2,1)S(1)}) custom-call(s32[4]{0:T(128)S(1)} %copy-done.25, bf16[128,9216]{1,0:T(8,128)(2,1)S(1)} %rotate_grad.1.mine_ref, bf16[128,9216]{1,0:T(8,128)(2,1)S(1)} %copy-done.1, bf16[4,288,512]{2,1,0:T(8,128)(2,1)S(1)} %copy-done.6, ...), custom_call_target="tpu_custom_call" | custom-call | flops 1073741824 | bytes 6291456 | tf_op jit(solution)/shard_map/pallas_call | solution.py:333
  202.4 4.6 %shard_map.87 = (f32[256,512]{1,0:T(8,128)S(1)}, f32[1,256,512]{2,1,0:T(8,128)S(1)}, bf16[1024,512]{1,0:T(8,128)(2,1)S(1)}) custom-call(s32[4]{0:T(128)S(1)} %copy-done.25, bf16[128,9216]{1,0:T(8,128)(2,1)S(1)} %rotate_grad.1.mine_ref, bf16[128,9216]{1,0:T(8,128)(2,1)S(1)} %copy-done.1, ...), custom_call_target="tpu_custom_call", output_to_operand_aliasing={{0}: (5, {}), {2}: (6, {})} | custom-call | flops 1073741824 | bytes 6291456 | tf_op jit(solution)/shard_map/pallas_call | solution.py:333
  207.0 3.5 %shard_map.88 = (f32[256,512]{1,0:T(8,128)S(1)}, f32[1,256,512]{2,1,0:T(8,128)S(1)}, bf16[1024,512]{1,0:T(8,128)(2,1)S(1)}) custom-call(s32[4]{0:T(128)S(1)} %copy-done.25, bf16[128,9216]{1,0:T(8,128)(2,1)S(1)} %rotate_grad.1.mine_ref, bf16[128,9216]{1,0:T(8,128)(2,1)S(1)} %copy-done.1, ...), custom_call_target="tpu_custom_call", output_to_operand_aliasing={{0}: (5, {}), {2}: (6, {})} | custom-call | flops 1073741824 | bytes 6291456 | tf_op jit(solution)/shard_map/pallas_call | solution.py:333
  210.5 3.1 %shard_map.90 = (f32[256,512]{1,0:T(8,128)S(1)}, f32[4,256,512]{2,1,0:T(8,128)S(1)}, bf16[1024,512]{1,0:T(8,128)(2,1)S(1)}) custom-call(s32[4]{0:T(128)S(1)} %copy-done.25, bf16[128,9216]{1,0:T(8,128)(2,1)S(1)} %rotate_grad.1.mine_ref, bf16[128,9216]{1,0:T(8,128)(2,1)S(1)} %copy-done.1, ...), custom_call_target="tpu_custom_call", output_to_operand_aliasing={{0}: (5, {}), {1}: (6, {}), {2}: (7, {})} | custom-call | flops 1073741824 | bytes 6291456 | tf_op jit(solution)/shard_map/pallas_call | solution.py:333
  213.7 4.6 %shard_map.91 = (f32[256,512]{1,0:T(8,128)S(1)}, f32[4,256,512]{2,1,0:T(8,128)S(1)}, bf16[1024,512]{1,0:T(8,128)(2,1)S(1)}) custom-call(s32[4]{0:T(128)S(1)} %copy-done.25, bf16[128,9216]{1,0:T(8,128)(2,1)S(1)} %rotate_grad.1.mine_ref, bf16[128,9216]{1,0:T(8,128)(2,1)S(1)} %copy-done.1, ...), custom_call_target="tpu_custom_call", output_to_operand_aliasing={{0}: (5, {}), {1}: (6, {}), {2}: (7, {})} | custom-call | flops 1073741824 | bytes 6291456 | tf_op jit(solution)/shard_map/pallas_call | solution.py:333
  218.3 14.1 %collective-permute-done.21.refs_3_ = bf16[4,288,512]{2,1,0:T(8,128)(2,1)} collective-permute-done((bf16[4,288,512]{2,1,0:T(8,128)(2,1)}, bf16[4,288,512]{2,1,0:T(8,128)(2,1)}, u32[]{:S(2)}, u32[]{:S(2)}) %collective-permute-start.21) | collective-permute-done | bytes 1179680 | tf_op jit(solution)/shard_map/ppermute | solution.py:446
  232.5 11.9 %last.1 = (f32[1024,256]{1,0:T(8,128)}, f32[4,1024]{1,0:T(4,128)S(1)}) custom-call(s32[4]{0:T(128)S(1)} %copy-done.25, f32[5]{0:T(128)S(1)} %pad_maximum_fusion.scale_ref, bf16[128,9216]{1,0:T(8,128)(2,1)S(1)} %rotate_grad.1.mine_ref, bf16[128,9216]{1,0:T(8,128)(2,1)S(1)} %copy-done.2, bf16[4,288,512]{2,1,0:T(8,128)(2,1)} %collective-permute-done.10.refs_0_, ...), custom_call_target="tpu_custom_call" | custom-call | tf_op jit(solution)/shard_map/last/pallas_call | solution.py:422
  244.7 3.9 %collective-permute-start.26 = (f32[2,128]{1,0:T(2,128)S(1)}, f32[2,128]{1,0:T(2,128)S(1)}, u32[]{:S(2)}, u32[]{:S(2)}) collective-permute-start(f32[2,128]{1,0:T(2,128)S(1)} %div.10), channel_id=1, source_target_pairs={{0,1},{1,0},{2,3},{3,2},{4,5},{5,4},{6,7},{7,6},{8,9},{9,8},{10,11... | collective-permute-start | bytes 3080 | tf_op jit(solution)/shard_map/ppermute | solution.py:505
  249.5 17.2 %all_to_all.10 = f32[128,2,128]{2,1,0:T(2,128)S(1)} all-to-all(f32[128,2,128]{2,1,0:T(2,128)S(1)} %broadcast_in_dim.10), channel_id=1, replica_groups=mesh['dp_0'=4,'dp_1'=4,'dp_2'=4,'mp_0'=2,'mp_1'=2] {'dp_0','dp_1','dp_2'..., dimensions={0} | all-to-all | bytes 262144 | tf_op jit(solution)/shard_map/all_to_all | solution.py:507
  (105 shorter events, 28.5 us)
Async XLA Ops:
  6.2 37.0 %all-to-all-start = ((bf16[16,360,128]{2,1,0:T(8,128)(2,1)}), bf16[16,360,128]{2,1,0:T(8,128)(2,1)S(1)}, u32[]{:S(2)}, u32[]{:S(2)}) async-start(bf16[16,360,128]{2,1,0:T(8,128)(2,1)} %pack.1), calls=%async_computation | async-start | bytes 2949120 | tf_op jit(solution)/shard_map/all_to_all | solution.py:481
  14.0 10.9 %collective-permute-start.5 = (bf16[144,1024]{1,0:T(8,128)(2,1)S(1)}, bf16[144,1024]{1,0:T(8,128)(2,1)S(1)}, u32[]{:S(2)}, u32[]{:S(2)}) collective-permute-start(bf16[144,1024]{1,0:T(8,128)(2,1)S(1)} %copy-done.11), channel_id=1, source_target_pairs={{0,4},{4,8},{8,12},{12,0},{1,5},{5,9},{9,13},{13,1},{2,6},{6,10},{... | collective-permute-start | bytes 884744 | tf_op jit(solution)/shard_map/ppermute | solution.py:446
  15.7 22.9 %collective-permute-start.6 = (bf16[144,1024]{1,0:T(8,128)(2,1)S(1)}, bf16[144,1024]{1,0:T(8,128)(2,1)S(1)}, u32[]{:S(2)}, u32[]{:S(2)}) collective-permute-start(bf16[144,1024]{1,0:T(8,128)(2,1)S(1)} %copy-done.11), channel_id=1, source_target_pairs={{0,8},{4,12},{8,0},{12,4},{1,9},{5,13},{9,1},{13,5},{2,10},{6,14},... | collective-permute-start | bytes 884744 | tf_op jit(solution)/shard_map/ppermute | solution.py:446
  18.7 19.9 %collective-permute-start.7 = (bf16[144,1024]{1,0:T(8,128)(2,1)S(1)}, bf16[144,1024]{1,0:T(8,128)(2,1)S(1)}, u32[]{:S(2)}, u32[]{:S(2)}) collective-permute-start(bf16[144,1024]{1,0:T(8,128)(2,1)S(1)} %copy-done.11), channel_id=1, source_target_pairs={{0,12},{4,0},{8,4},{12,8},{1,13},{5,1},{9,5},{13,9},{2,14},{6,2},{... | collective-permute-start | bytes 884744 | tf_op jit(solution)/shard_map/ppermute | solution.py:446
  39.5 66.5 %copy-start.20 = (bf16[2,288,512]{2,1,0:T(8,128)(2,1)}, bf16[2,288,512]{2,1,0:T(8,128)(2,1)S(1)}, u32[]{:S(2)}) copy-start(bf16[2,288,512]{2,1,0:T(8,128)(2,1)S(1)} %get-tuple-element.25.refs_0_) | copy-start | bytes 1769476
  39.5 14.9 %collective-permute-start.18 = (bf16[2,288,512]{2,1,0:T(8,128)(2,1)S(1)}, bf16[2,288,512]{2,1,0:T(8,128)(2,1)}, u32[]{:S(2)}, u32[]{:S(2)}) collective-permute-start(bf16[2,288,512]{2,1,0:T(8,128)(2,1)S(1)} %get-tuple-element.25.refs_0_), channel_id=1, source_target_pairs={{0,192},{64,0},{128,64},{192,128},{1,193},{65,1},{129,65},{193,129... | collective-permute-start | bytes 1769480 | tf_op jit(solution)/shard_map/ppermute | solution.py:446
  42.1 15.2 %collective-permute-start.15 = (bf16[2,288,512]{2,1,0:T(8,128)(2,1)S(1)}, bf16[2,288,512]{2,1,0:T(8,128)(2,1)S(1)}, u32[]{:S(2)}, u32[]{:S(2)}) collective-permute-start(bf16[2,288,512]{2,1,0:T(8,128)(2,1)S(1)} %get-tuple-element.25.refs_0_), channel_id=1, source_target_pairs={{0,64},{64,128},{128,192},{192,0},{1,65},{65,129},{129,193},{193,1... | collective-permute-start | bytes 1769480 | tf_op jit(solution)/shard_map/ppermute | solution.py:446
  42.1 21.7 %collective-permute-start.8 = (bf16[2,288,512]{2,1,0:T(8,128)(2,1)}, bf16[2,288,512]{2,1,0:T(8,128)(2,1)S(1)}, u32[]{:S(2)}, u32[]{:S(2)}) collective-permute-start(bf16[2,288,512]{2,1,0:T(8,128)(2,1)} %get-tuple-element.24.refs_0_), channel_id=1, source_target_pairs={{0,16},{16,32},{32,48},{48,0},{1,17},{17,33},{33,49},{49,1},{2,18}... | collective-permute-start | bytes 1769480 | tf_op jit(solution)/shard_map/ppermute | solution.py:446
  43.3 67.8 %copy-start.3 = (bf16[16,360,128]{2,1,0:T(8,128)(2,1)}, bf16[16,360,128]{2,1,0:T(8,128)(2,1)S(1)}, u32[]{:S(2)}) copy-start(bf16[16,360,128]{2,1,0:T(8,128)(2,1)S(1)} %all-to-all-done.own_ref) | copy-start | bytes 4423684
  43.3 69.0 %collective-permute-start = (bf16[16,144,128]{2,1,0:T(8,128)(2,1)S(1)}, bf16[16,144,128]{2,1,0:T(8,128)(2,1)S(1)}, u32[]{:S(2)}, u32[]{:S(2)}) collective-permute-start(bf16[16,144,128]{2,1,0:T(8,128)(2,1)S(1)} %slice.8), channel_id=1, source_target_pairs={{0,4},{4,8},{8,12},{12,2},{2,14},{6,0},{10,6},{14,10},{1,5},{5,9},... | collective-permute-start | bytes 1769480 | tf_op jit(solution)/shard_map/ppermute | solution.py:467
  50.0 65.0 %collective-permute-start.1 = (bf16[16,144,128]{2,1,0:T(8,128)(2,1)S(1)}, bf16[16,144,128]{2,1,0:T(8,128)(2,1)S(1)}, u32[]{:S(2)}, u32[]{:S(2)}) collective-permute-start(bf16[16,144,128]{2,1,0:T(8,128)(2,1)S(1)} %slice.8), channel_id=1, source_target_pairs={{0,6},{4,10},{8,14},{12,0},{2,12},{6,2},{10,4},{14,8},{1,7},{5,11}... | collective-permute-start | bytes 1769480 | tf_op jit(solution)/shard_map/ppermute | solution.py:467
  54.4 66.8 %collective-permute-start.12 = (bf16[2,288,512]{2,1,0:T(8,128)(2,1)}, bf16[2,288,512]{2,1,0:T(8,128)(2,1)S(1)}, u32[]{:S(2)}, u32[]{:S(2)}) collective-permute-start(bf16[2,288,512]{2,1,0:T(8,128)(2,1)} %get-tuple-element.24.refs_0_), channel_id=1, source_target_pairs={{0,48},{16,0},{32,16},{48,32},{1,49},{17,1},{33,17},{49,33},{2,50}... | collective-permute-start | bytes 1769480 | tf_op jit(solution)/shard_map/ppermute | solution.py:446
  58.1 47.9 %collective-permute-start.2 = (bf16[16,72,128]{2,1,0:T(8,128)(2,1)S(1)}, bf16[16,72,128]{2,1,0:T(8,128)(2,1)S(1)}, u32[]{:S(2)}, u32[]{:S(2)}) collective-permute-start(bf16[16,72,128]{2,1,0:T(8,128)(2,1)S(1)} %slice.9), channel_id=1, source_target_pairs={{0,8},{4,12},{8,2},{12,6},{2,10},{6,14},{10,0},{14,4},{1,9},{5,13}... | collective-permute-start | bytes 884744 | tf_op jit(solution)/shard_map/ppermute | solution.py:467
  63.8 48.4 %collective-permute-start.3 = (bf16[16,72,128]{2,1,0:T(8,128)(2,1)S(1)}, bf16[16,72,128]{2,1,0:T(8,128)(2,1)S(1)}, u32[]{:S(2)}, u32[]{:S(2)}) collective-permute-start(bf16[16,72,128]{2,1,0:T(8,128)(2,1)S(1)} %slice.9), channel_id=1, source_target_pairs={{0,10},{4,14},{8,0},{12,4},{2,8},{6,12},{10,2},{14,6},{1,11},{5,15... | collective-permute-start | bytes 884744 | tf_op jit(solution)/shard_map/ppermute | solution.py:467
  106.0 17.0 %collective-permute-start.19 = (bf16[2,288,512]{2,1,0:T(8,128)(2,1)}, bf16[2,288,512]{2,1,0:T(8,128)(2,1)S(1)}, u32[]{:S(2)}, u32[]{:S(2)}) collective-permute-start(bf16[2,288,512]{2,1,0:T(8,128)(2,1)} %collective-permute-done.18.refs_1_), channel_id=1, source_target_pairs={{0,192},{64,0},{128,64},{192,128},{1,193},{65,1},{129,65},{193,129... | collective-permute-start | bytes 1769480 | tf_op jit(solution)/shard_map/ppermute | solution.py:446
  112.2 45.8 %collective-permute-start.9 = (bf16[4,288,512]{2,1,0:T(8,128)(2,1)S(1)}, bf16[4,288,512]{2,1,0:T(8,128)(2,1)}, u32[]{:S(2)}, u32[]{:S(2)}) collective-permute-start(bf16[4,288,512]{2,1,0:T(8,128)(2,1)S(1)} %join.4.p_ref), channel_id=1, source_target_pairs={{0,64},{64,128},{128,192},{192,0},{1,65},{65,129},{129,193},{193,1... | collective-permute-start | bytes 3538952 | tf_op jit(solution)/shard_map/ppermute | solution.py:446
  112.4 45.7 %collective-permute-start.22 = (bf16[4,288,512]{2,1,0:T(8,128)(2,1)S(1)}, bf16[4,288,512]{2,1,0:T(8,128)(2,1)S(1)}, u32[]{:S(2)}, u32[]{:S(2)}) collective-permute-start(bf16[4,288,512]{2,1,0:T(8,128)(2,1)S(1)} %join.4.p_ref), channel_id=1, source_target_pairs={{0,192},{64,0},{128,64},{192,128},{1,193},{65,1},{129,65},{193,129... | collective-permute-start | bytes 3538952 | tf_op jit(solution)/shard_map/ppermute | solution.py:446
  115.0 40.3 %collective-permute-start.16 = (bf16[4,288,512]{2,1,0:T(8,128)(2,1)S(1)}, bf16[4,288,512]{2,1,0:T(8,128)(2,1)}, u32[]{:S(2)}, u32[]{:S(2)}) collective-permute-start(bf16[4,288,512]{2,1,0:T(8,128)(2,1)S(1)} %join.6.p_ref), channel_id=1, source_target_pairs={{0,16},{16,32},{32,48},{48,0},{1,17},{17,33},{33,49},{49,1},{2,18}... | collective-permute-start | bytes 3538952 | tf_op jit(solution)/shard_map/ppermute | solution.py:446
  121.3 66.5 %collective-permute-start.4 = (bf16[128,9216]{1,0:T(8,128)(2,1)S(1)}, bf16[128,9216]{1,0:T(8,128)(2,1)S(1)}, u32[]{:S(2)}, u32[]{:S(2)}) collective-permute-start(bf16[128,9216]{1,0:T(8,128)(2,1)S(1)} %rotate_grad.1.mine_ref), channel_id=1, source_target_pairs={{0,1},{1,0},{2,3},{3,2},{4,5},{5,4},{6,7},{7,6},{8,9},{9,8},{10,11... | collective-permute-start | bytes 7077896 | tf_op jit(solution)/shard_map/ppermute | solution.py:485
  123.0 32.0 %collective-permute-start.11 = (bf16[2,288,512]{2,1,0:T(8,128)(2,1)S(1)}, bf16[2,288,512]{2,1,0:T(8,128)(2,1)S(1)}, u32[]{:S(2)}, u32[]{:S(2)}) collective-permute-start(bf16[2,288,512]{2,1,0:T(8,128)(2,1)S(1)} %copy-done.19), channel_id=1, source_target_pairs={{0,16},{16,32},{32,48},{48,0},{1,17},{17,33},{33,49},{49,1},{2,18}... | collective-permute-start | bytes 1769480 | tf_op jit(solution)/shard_map/ppermute | solution.py:446
  125.2 62.6 %copy-start.7 = (bf16[4,288,512]{2,1,0:T(8,128)(2,1)}, bf16[4,288,512]{2,1,0:T(8,128)(2,1)S(1)}, u32[]{:S(2)}) copy-start(bf16[4,288,512]{2,1,0:T(8,128)(2,1)S(1)} %join.7.q_ref) | copy-start | bytes 3538948
  125.2 65.2 %copy-start.25 = (s32[4]{0:T(128)S(1)}, s32[4]{0:T(128)}, u32[]{:S(2)}) copy-start(s32[4]{0:T(128)} %len_ref.15) | copy-start | bytes 52
  155.1 26.5 %collective-permute-start.25 = (bf16[4,288,512]{2,1,0:T(8,128)(2,1)S(1)}, bf16[4,288,512]{2,1,0:T(8,128)(2,1)S(1)}, u32[]{:S(2)}, u32[]{:S(2)}) collective-permute-start(bf16[4,288,512]{2,1,0:T(8,128)(2,1)S(1)} %join.7.q_ref), channel_id=1, source_target_pairs={{0,16},{16,32},{32,48},{48,0},{1,17},{17,33},{33,49},{49,1},{2,18}... | collective-permute-start | bytes 3538952 | tf_op jit(solution)/shard_map/ppermute | solution.py:446
  155.3 27.3 %collective-permute-start.20 = (bf16[4,288,512]{2,1,0:T(8,128)(2,1)S(1)}, bf16[4,288,512]{2,1,0:T(8,128)(2,1)}, u32[]{:S(2)}, u32[]{:S(2)}) collective-permute-start(bf16[4,288,512]{2,1,0:T(8,128)(2,1)S(1)} %join.7.q_ref), channel_id=1, source_target_pairs={{0,48},{16,0},{32,16},{48,32},{1,49},{17,1},{33,17},{49,33},{2,50}... | collective-permute-start | bytes 3538952 | tf_op jit(solution)/shard_map/ppermute | solution.py:446
  158.1 26.0 %collective-permute-start.23 = (bf16[4,288,512]{2,1,0:T(8,128)(2,1)S(1)}, bf16[4,288,512]{2,1,0:T(8,128)(2,1)S(1)}, u32[]{:S(2)}, u32[]{:S(2)}) collective-permute-start(bf16[4,288,512]{2,1,0:T(8,128)(2,1)S(1)} %join.5.q_ref), channel_id=1, source_target_pairs={{0,64},{64,128},{128,192},{192,0},{1,65},{65,129},{129,193},{193,1... | collective-permute-start | bytes 3538952 | tf_op jit(solution)/shard_map/ppermute | solution.py:446
  159.1 26.0 %collective-permute-start.13 = (bf16[4,288,512]{2,1,0:T(8,128)(2,1)S(1)}, bf16[4,288,512]{2,1,0:T(8,128)(2,1)}, u32[]{:S(2)}, u32[]{:S(2)}) collective-permute-start(bf16[4,288,512]{2,1,0:T(8,128)(2,1)S(1)} %join.5.q_ref), channel_id=1, source_target_pairs={{0,192},{64,0},{128,64},{192,128},{1,193},{65,1},{129,65},{193,129... | collective-permute-start | bytes 3538952 | tf_op jit(solution)/shard_map/ppermute | solution.py:446
  182.6 31.0 %collective-permute-start.24 = (bf16[4,288,512]{2,1,0:T(8,128)(2,1)S(1)}, bf16[4,288,512]{2,1,0:T(8,128)(2,1)}, u32[]{:S(2)}, u32[]{:S(2)}) collective-permute-start(bf16[4,288,512]{2,1,0:T(8,128)(2,1)S(1)} %join.6.p_ref), channel_id=1, source_target_pairs={{0,48},{16,0},{32,16},{48,32},{1,49},{17,1},{33,17},{49,33},{2,50}... | collective-permute-start | bytes 3538952 | tf_op jit(solution)/shard_map/ppermute | solution.py:446
  182.6 35.7 %collective-permute-start.10 = (bf16[4,288,512]{2,1,0:T(8,128)(2,1)}, bf16[4,288,512]{2,1,0:T(8,128)(2,1)}, u32[]{:S(2)}, u32[]{:S(2)}) collective-permute-start(bf16[4,288,512]{2,1,0:T(8,128)(2,1)} %collective-permute-done.9.p_ref), channel_id=1, source_target_pairs={{0,64},{64,128},{128,192},{192,0},{1,65},{65,129},{129,193},{193,1... | collective-permute-start | bytes 3538952 | tf_op jit(solution)/shard_map/ppermute | solution.py:446
  185.1 33.2 %collective-permute-start.17 = (bf16[4,288,512]{2,1,0:T(8,128)(2,1)}, bf16[4,288,512]{2,1,0:T(8,128)(2,1)}, u32[]{:S(2)}, u32[]{:S(2)}) collective-permute-start(bf16[4,288,512]{2,1,0:T(8,128)(2,1)} %collective-permute-done.16.p_ref), channel_id=1, source_target_pairs={{0,16},{16,32},{32,48},{48,0},{1,17},{17,33},{33,49},{49,1},{2,18}... | collective-permute-start | bytes 3538952 | tf_op jit(solution)/shard_map/ppermute | solution.py:446
  185.1 47.4 %collective-permute-start.21 = (bf16[4,288,512]{2,1,0:T(8,128)(2,1)}, bf16[4,288,512]{2,1,0:T(8,128)(2,1)}, u32[]{:S(2)}, u32[]{:S(2)}) collective-permute-start(bf16[4,288,512]{2,1,0:T(8,128)(2,1)} %collective-permute-done.20.q_ref), channel_id=1, source_target_pairs={{0,48},{16,0},{32,16},{48,32},{1,49},{17,1},{33,17},{49,33},{2,50}... | collective-permute-start | bytes 3538952 | tf_op jit(solution)/shard_map/ppermute | solution.py:446
  189.2 43.3 %collective-permute-start.14 = (bf16[4,288,512]{2,1,0:T(8,128)(2,1)}, bf16[4,288,512]{2,1,0:T(8,128)(2,1)}, u32[]{:S(2)}, u32[]{:S(2)}) collective-permute-start(bf16[4,288,512]{2,1,0:T(8,128)(2,1)} %collective-permute-done.13.q_ref), channel_id=1, source_target_pairs={{0,192},{64,0},{128,64},{192,128},{1,193},{65,1},{129,65},{193,129... | collective-permute-start | bytes 3538952 | tf_op jit(solution)/shard_map/ppermute | solution.py:446
  244.7 4.7 %collective-permute-start.26 = (f32[2,128]{1,0:T(2,128)S(1)}, f32[2,128]{1,0:T(2,128)S(1)}, u32[]{:S(2)}, u32[]{:S(2)}) collective-permute-start(f32[2,128]{1,0:T(2,128)S(1)} %div.10), channel_id=1, source_target_pairs={{0,1},{1,0},{2,3},{3,2},{4,5},{5,4},{6,7},{7,6},{8,9},{9,8},{10,11... | collective-permute-start | bytes 3080 | tf_op jit(solution)/shard_map/ppermute | solution.py:505
  (22 other events, 127.1 us)

commit v2 on v1

--- a/solution.py
+++ b/solution.py
@@ -337,7 +337,7 @@
             jax.ShapeDtypeStruct((seq_rows, COLS, HALF), jnp.float32),
             jax.ShapeDtypeStruct((QROWS, HALF), jnp.bfloat16),
         ),
-        in_specs=[spec(SM)] + [spec(ANY)] * 4 + [spec(VM)] * len(carried),
+        in_specs=[spec(SM)] + [spec(pltpu.HBM)] * 2 + [spec(ANY)] * 2 + [spec(VM)] * len(carried),
         out_specs=(spec(VM),) * 3,
         scratch_shapes=[
             pltpu.VMEM((HALVES, 2 * ROWS, HALF), jnp.bfloat16),
@@ -360,7 +360,7 @@
 def last_kernel(len_ref, scale_ref, mine_ref, other_ref, *refs):
     pairs, refs = (refs[0:2], refs[2:4]), refs[4:]
     moms, seq_a, seq_b, q_ins, refs = refs[0:2], refs[2:5], refs[5], refs[6:8], refs[8:]
-    out_ref, score_ref, w_ref, s_ref, q_ref, u_ref, g_ref, qg_ref, p_ref, sem = refs
+    moments_ref, score_ref, w_ref, s_ref, q_ref, u_ref, g_ref, qg_ref, p_ref, out_ref, sem = refs
     y, _, _, _, c = where()
     copies = [
         group_copies(part, FAR, pairs[part], (mine_ref, other_ref), u_ref.at[part], g_ref.at[part], sem.at[part])
@@ -402,6 +402,9 @@
         out_ref[rows, pl.ds(other_at, BLOCK)] = m[BLOCK:COLS, :].T
         w_ref[part, :, cols] = 1.0 / (m + damping)
 
+    leave = pltpu.make_async_copy(out_ref, moments_ref, sem.at[2, 2])
+    leave.start()
+
     @pl.loop(0, SEQS)
     def _(s):
         for part in range(2):
@@ -417,6 +420,8 @@
             total += jnp.sum(mapped[BLOCK:COLS] * qg_ref[1, :, rows].astype(jnp.float32), axis=0, keepdims=True)
             score_ref[pl.ds(s, 1), rows] = total
 
+    leave.wait()
+
 
 def last(lengths, scales, mine, other, pairs, carried):
     return pl.pallas_call(
@@ -425,8 +430,8 @@
             jax.ShapeDtypeStruct((FEAT, COLS), jnp.float32),
             jax.ShapeDtypeStruct((SEQS, QROWS), jnp.float32),
         ),
-        in_specs=[spec(SM)] * 2 + [spec(ANY)] * 6 + [spec(VM)] * len(carried),
-        out_specs=(spec(VM), spec(VM)),
+        in_specs=[spec(SM)] * 2 + [spec(pltpu.HBM)] * 2 + [spec(ANY)] * 4 + [spec(VM)] * len(carried),
+        out_specs=(spec(pltpu.HBM), spec(VM)),
         scratch_shapes=[
             pltpu.VMEM((2, COLS, HALF), jnp.float32),
             pltpu.VMEM((2, SEQS, COLS, HALF), jnp.float32),
@@ -435,6 +440,7 @@
             pltpu.VMEM((2, 2, BLOCK, SEQ_LEN), jnp.bfloat16),
             pltpu.VMEM((2, BLOCK, QROWS), jnp.bfloat16),
             pltpu.VMEM((2, COLS, HALF), jnp.bfloat16),
+            pltpu.VMEM((FEAT, COLS), jnp.float32),
             pltpu.SemaphoreType.DMA((3, SEMS)),
         ],
         compiler_params=pltpu.CompilerParams(vmem_limit_bytes=32 << 20),

time: 268 us -> 267 us (level)
  no operation moved by 1% of the time
where the time goes in v2:
time: 267 us
  waiting for transfers between devices  124 us (46%)
  starting transfers between devices  61.7 us (23%)
  Pallas kernels  47.4 us (18%)
  blocking collectives  17.2 us (6%)
  local copies, waits for them, and re-layouts  13.7 us (5%)
    ppermute x21, waiting for transfers between devices, shift(): return lax.ppermute(x, axis, [(i, (i + step) % RING) for i in range(RING)])  84.1 us
    ppermute x4, waiting for transfers between devices, along_z(): return lax.ppermute(x, (Z, H), [(at_z(a), at_z(b)) for a, b in pairs])  38.8 us
    ppermute x21, starting transfers between devices, shift(): return lax.ppermute(x, axis, [(i, (i + step) % RING) for i in range(RING)])  28.1 us
    pallas_call x6, Pallas kernels, group(): pl.pallas_call(functools.partial(group_kernel, part, outer), out_shape=(j...  23.4 us
    ppermute x4, starting transfers between devices, along_z(): return lax.ppermute(x, (Z, H), [(at_z(a), at_z(b)) for a, b in pairs])  20.2 us
    all_to_all x1, blocking collectives, local(): scores = lax.all_to_all(everywhere, (Y, X, Z, H), 0, 0, tiled=True).sum(0)  17.2 us
    unnamed x52, local copies, waits for them, and re-layouts  12.8 us
    pallas_call x1, Pallas kernels, last(): pl.pallas_call(last_kernel, out_shape=(jax.ShapeDtypeStruct((FEAT, COLS),...  10.9 us
  transfers between devices with their start and end apart: 28, of which 9 were waited for; matrix products, arithmetic and copies ran while one was open for 0% of the time, Pallas kernels for 12%

profile of v2, /device:TPU:1, one launch (start us, length us, event | category | flops | bytes accessed | tf_op | source)
XLA Modules:
  0.0 266.6 jit_solution(8981533514563399355)
XLA Ops:
  0.6 2.0 rotate_act.1.after_ref.refs_0_
  2.7 3.6 %pack.1 = bf16[16,360,128]{2,1,0:T(8,128)(2,1)} custom-call(bf16[128,16384]{1,0:T(8,128)(2,1)} %g_ref.1, bf16[16,16384]{1,0:T(8,128)(2,1)} %q_ref.3, bf16[144,1024]{1,0:T(8,128)(2,1)} %rotate_act.1.after_ref.refs_0_), custom_call_target="tpu_custom_call" | custom-call | tf_op jit(solution)/shard_map/pack/pallas_call | solution.py:138
  6.2 7.7 %all-to-all-start = ((bf16[16,360,128]{2,1,0:T(8,128)(2,1)}), bf16[16,360,128]{2,1,0:T(8,128)(2,1)S(1)}, u32[]{:S(2)}, u32[]{:S(2)}) async-start(bf16[16,360,128]{2,1,0:T(8,128)(2,1)} %pack.1), calls=%async_computation | async-start | bytes 2949120 | tf_op jit(solution)/shard_map/all_to_all | solution.py:487
  15.7 3.0 %collective-permute-start.6 = (bf16[144,1024]{1,0:T(8,128)(2,1)S(1)}, bf16[144,1024]{1,0:T(8,128)(2,1)S(1)}, u32[]{:S(2)}, u32[]{:S(2)}) collective-permute-start(bf16[144,1024]{1,0:T(8,128)(2,1)S(1)} %copy-done.11), channel_id=1, source_target_pairs={{0,8},{4,12},{8,0},{12,4},{1,9},{5,13},{9,1},{13,5},{2,10},{6,14},... | collective-permute-start | bytes 884744 | tf_op jit(solution)/shard_map/ppermute | solution.py:452
  19.4 5.5 %collective-permute-done.5.refs_1_ = bf16[144,1024]{1,0:T(8,128)(2,1)S(1)} collective-permute-done((bf16[144,1024]{1,0:T(8,128)(2,1)S(1)}, bf16[144,1024]{1,0:T(8,128)(2,1)S(1)}, u32[]{:S(2)}, u32[]{:S(2)}) %collective-permute-start.5) | collective-permute-done | bytes 294944 | tf_op jit(solution)/shard_map/ppermute | solution.py:452
  24.9 13.6 %collective-permute-done.6.refs_2_ = bf16[144,1024]{1,0:T(8,128)(2,1)S(1)} collective-permute-done((bf16[144,1024]{1,0:T(8,128)(2,1)S(1)}, bf16[144,1024]{1,0:T(8,128)(2,1)S(1)}, u32[]{:S(2)}, u32[]{:S(2)}) %collective-permute-start.6) | collective-permute-done | bytes 294944 | tf_op jit(solution)/shard_map/ppermute | solution.py:452
  39.5 2.6 collective-permute-start.18
  43.3 6.7 %collective-permute-start = (bf16[16,144,128]{2,1,0:T(8,128)(2,1)S(1)}, bf16[16,144,128]{2,1,0:T(8,128)(2,1)S(1)}, u32[]{:S(2)}, u32[]{:S(2)}) collective-permute-start(bf16[16,144,128]{2,1,0:T(8,128)(2,1)S(1)} %slice.8), channel_id=1, source_target_pairs={{0,4},{4,8},{8,12},{12,2},{2,14},{6,0},{10,6},{14,10},{1,5},{5,9},... | collective-permute-start | bytes 1769480 | tf_op jit(solution)/shard_map/ppermute | solution.py:473
  50.0 4.4 %collective-permute-start.1 = (bf16[16,144,128]{2,1,0:T(8,128)(2,1)S(1)}, bf16[16,144,128]{2,1,0:T(8,128)(2,1)S(1)}, u32[]{:S(2)}, u32[]{:S(2)}) collective-permute-start(bf16[16,144,128]{2,1,0:T(8,128)(2,1)S(1)} %slice.8), channel_id=1, source_target_pairs={{0,6},{4,10},{8,14},{12,0},{2,12},{6,2},{10,4},{14,8},{1,7},{5,11}... | collective-permute-start | bytes 1769480 | tf_op jit(solution)/shard_map/ppermute | solution.py:473
  54.4 2.1 collective-permute-start.12
  58.1 5.7 %collective-permute-start.2 = (bf16[16,72,128]{2,1,0:T(8,128)(2,1)S(1)}, bf16[16,72,128]{2,1,0:T(8,128)(2,1)S(1)}, u32[]{:S(2)}, u32[]{:S(2)}) collective-permute-start(bf16[16,72,128]{2,1,0:T(8,128)(2,1)S(1)} %slice.9), channel_id=1, source_target_pairs={{0,8},{4,12},{8,2},{12,6},{2,10},{6,14},{10,0},{14,4},{1,9},{5,13}... | collective-permute-start | bytes 884744 | tf_op jit(solution)/shard_map/ppermute | solution.py:473
  63.8 3.4 %collective-permute-start.3 = (bf16[16,72,128]{2,1,0:T(8,128)(2,1)S(1)}, bf16[16,72,128]{2,1,0:T(8,128)(2,1)S(1)}, u32[]{:S(2)}, u32[]{:S(2)}) collective-permute-start(bf16[16,72,128]{2,1,0:T(8,128)(2,1)S(1)} %slice.9), channel_id=1, source_target_pairs={{0,10},{4,14},{8,0},{12,4},{2,8},{6,12},{10,2},{14,6},{1,11},{5,15... | collective-permute-start | bytes 884744 | tf_op jit(solution)/shard_map/ppermute | solution.py:473
  67.2 38.8 %collective-permute-done.2.f1_ref = bf16[16,72,128]{2,1,0:T(8,128)(2,1)S(1)} collective-permute-done((bf16[16,72,128]{2,1,0:T(8,128)(2,1)S(1)}, bf16[16,72,128]{2,1,0:T(8,128)(2,1)S(1)}, u32[]{:S(2)}, u32[]{:S(2)}) %collective-permute-start.2) | collective-permute-done | bytes 294944 | tf_op jit(solution)/shard_map/ppermute | solution.py:473
  106.0 2.7 %collective-permute-start.19 = (bf16[2,288,512]{2,1,0:T(8,128)(2,1)}, bf16[2,288,512]{2,1,0:T(8,128)(2,1)S(1)}, u32[]{:S(2)}, u32[]{:S(2)}) collective-permute-start(bf16[2,288,512]{2,1,0:T(8,128)(2,1)} %collective-permute-done.18.refs_1_), channel_id=1, source_target_pairs={{0,192},{64,0},{128,64},{192,128},{1,193},{65,1},{129,65},{193,129... | collective-permute-start | bytes 1769480 | tf_op jit(solution)/shard_map/ppermute | solution.py:452
  112.4 2.7 collective-permute-start.22
  117.5 3.7 %rotate_grad.1.mine_ref = bf16[128,9216]{1,0:T(8,128)(2,1)S(1)} custom-call(bf16[16,360,128]{2,1,0:T(8,128)(2,1)S(1)} %copy-done.4, bf16[16,144,128]{2,1,0:T(8,128)(2,1)S(1)} %collective-permute-done.u1_ref, bf16[16,144,128]{2,1,0:T(8,128)(2,1)S(1)} %collective-permute-done.1.u2_ref, bf16[16,72,128]{2,1,0:T(8,128)(2,1)S(1)} %collective-permute-done.2.f1_ref, ...), custom_call_target="tpu_custom_call" | custom-call | flops 301989888 | bytes 5242880 | tf_op jit(solution)/shard_map/rotate_grad/pallas_call | solution.py:187
  121.3 1.7 collective-permute-start.4
  125.2 29.9 %collective-permute-done.11.refs_0_ = bf16[2,288,512]{2,1,0:T(8,128)(2,1)S(1)} collective-permute-done((bf16[2,288,512]{2,1,0:T(8,128)(2,1)S(1)}, bf16[2,288,512]{2,1,0:T(8,128)(2,1)S(1)}, u32[]{:S(2)}, u32[]{:S(2)}) %collective-permute-start.11) | collective-permute-done | bytes 589856 | tf_op jit(solution)/shard_map/ppermute | solution.py:452
  155.3 2.8 %collective-permute-start.20 = (bf16[4,288,512]{2,1,0:T(8,128)(2,1)S(1)}, bf16[4,288,512]{2,1,0:T(8,128)(2,1)}, u32[]{:S(2)}, u32[]{:S(2)}) collective-permute-start(bf16[4,288,512]{2,1,0:T(8,128)(2,1)S(1)} %join.7.q_ref), channel_id=1, source_target_pairs={{0,48},{16,0},{32,16},{48,32},{1,49},{17,1},{33,17},{49,33},{2,50}... | collective-permute-start | bytes 3538952 | tf_op jit(solution)/shard_map/ppermute | solution.py:452
  159.1 2.7 %collective-permute-start.13 = (bf16[4,288,512]{2,1,0:T(8,128)(2,1)S(1)}, bf16[4,288,512]{2,1,0:T(8,128)(2,1)}, u32[]{:S(2)}, u32[]{:S(2)}) collective-permute-start(bf16[4,288,512]{2,1,0:T(8,128)(2,1)S(1)} %join.5.q_ref), channel_id=1, source_target_pairs={{0,192},{64,0},{128,64},{192,128},{1,193},{65,1},{129,65},{193,129... | collective-permute-start | bytes 3538952 | tf_op jit(solution)/shard_map/ppermute | solution.py:452
  162.8 18.8 %collective-permute-done.25.q_ref = bf16[4,288,512]{2,1,0:T(8,128)(2,1)S(1)} collective-permute-done((bf16[4,288,512]{2,1,0:T(8,128)(2,1)S(1)}, bf16[4,288,512]{2,1,0:T(8,128)(2,1)S(1)}, u32[]{:S(2)}, u32[]{:S(2)}) %collective-permute-start.25) | collective-permute-done | bytes 1179680 | tf_op jit(solution)/shard_map/ppermute | solution.py:452
  185.1 2.7 collective-permute-start.21
  194.7 4.0 %shard_map.89 = (f32[256,512]{1,0:T(8,128)S(1)}, f32[4,256,512]{2,1,0:T(8,128)S(1)}, bf16[1024,512]{1,0:T(8,128)(2,1)S(1)}) custom-call(s32[4]{0:T(128)S(1)} %copy-done.25, bf16[128,9216]{1,0:T(8,128)(2,1)S(1)} %rotate_grad.1.mine_ref, bf16[128,9216]{1,0:T(8,128)(2,1)S(1)} %copy-done.1, bf16[4,288,512]{2,1,0:T(8,128)(2,1)S(1)} %join.6.p_ref, ...), custom_call_target="tpu_custom_call" | custom-call | flops 1073741824 | bytes 6291456 | tf_op jit(solution)/shard_map/pallas_call | solution.py:333
  198.8 3.5 %shard_map.86 = (f32[256,512]{1,0:T(8,128)S(1)}, f32[1,256,512]{2,1,0:T(8,128)S(1)}, bf16[1024,512]{1,0:T(8,128)(2,1)S(1)}) custom-call(s32[4]{0:T(128)S(1)} %copy-done.25, bf16[128,9216]{1,0:T(8,128)(2,1)S(1)} %rotate_grad.1.mine_ref, bf16[128,9216]{1,0:T(8,128)(2,1)S(1)} %copy-done.1, bf16[4,288,512]{2,1,0:T(8,128)(2,1)S(1)} %copy-done.6, ...), custom_call_target="tpu_custom_call" | custom-call | flops 1073741824 | bytes 6291456 | tf_op jit(solution)/shard_map/pallas_call | solution.py:333
  202.4 4.6 %shard_map.87 = (f32[256,512]{1,0:T(8,128)S(1)}, f32[1,256,512]{2,1,0:T(8,128)S(1)}, bf16[1024,512]{1,0:T(8,128)(2,1)S(1)}) custom-call(s32[4]{0:T(128)S(1)} %copy-done.25, bf16[128,9216]{1,0:T(8,128)(2,1)S(1)} %rotate_grad.1.mine_ref, bf16[128,9216]{1,0:T(8,128)(2,1)S(1)} %copy-done.1, ...), custom_call_target="tpu_custom_call", output_to_operand_aliasing={{0}: (5, {}), {2}: (6, {})} | custom-call | flops 1073741824 | bytes 6291456 | tf_op jit(solution)/shard_map/pallas_call | solution.py:333
  207.0 3.5 %shard_map.88 = (f32[256,512]{1,0:T(8,128)S(1)}, f32[1,256,512]{2,1,0:T(8,128)S(1)}, bf16[1024,512]{1,0:T(8,128)(2,1)S(1)}) custom-call(s32[4]{0:T(128)S(1)} %copy-done.25, bf16[128,9216]{1,0:T(8,128)(2,1)S(1)} %rotate_grad.1.mine_ref, bf16[128,9216]{1,0:T(8,128)(2,1)S(1)} %copy-done.1, ...), custom_call_target="tpu_custom_call", output_to_operand_aliasing={{0}: (5, {}), {2}: (6, {})} | custom-call | flops 1073741824 | bytes 6291456 | tf_op jit(solution)/shard_map/pallas_call | solution.py:333
  210.5 3.1 %shard_map.90 = (f32[256,512]{1,0:T(8,128)S(1)}, f32[4,256,512]{2,1,0:T(8,128)S(1)}, bf16[1024,512]{1,0:T(8,128)(2,1)S(1)}) custom-call(s32[4]{0:T(128)S(1)} %copy-done.25, bf16[128,9216]{1,0:T(8,128)(2,1)S(1)} %rotate_grad.1.mine_ref, bf16[128,9216]{1,0:T(8,128)(2,1)S(1)} %copy-done.1, ...), custom_call_target="tpu_custom_call", output_to_operand_aliasing={{0}: (5, {}), {1}: (6, {}), {2}: (7, {})} | custom-call | flops 1073741824 | bytes 6291456 | tf_op jit(solution)/shard_map/pallas_call | solution.py:333
  213.7 4.6 %shard_map.91 = (f32[256,512]{1,0:T(8,128)S(1)}, f32[4,256,512]{2,1,0:T(8,128)S(1)}, bf16[1024,512]{1,0:T(8,128)(2,1)S(1)}) custom-call(s32[4]{0:T(128)S(1)} %copy-done.25, bf16[128,9216]{1,0:T(8,128)(2,1)S(1)} %rotate_grad.1.mine_ref, bf16[128,9216]{1,0:T(8,128)(2,1)S(1)} %copy-done.1, ...), custom_call_target="tpu_custom_call", output_to_operand_aliasing={{0}: (5, {}), {1}: (6, {}), {2}: (7, {})} | custom-call | flops 1073741824 | bytes 6291456 | tf_op jit(solution)/shard_map/pallas_call | solution.py:333
  218.3 14.1 %collective-permute-done.21.refs_3_ = bf16[4,288,512]{2,1,0:T(8,128)(2,1)} collective-permute-done((bf16[4,288,512]{2,1,0:T(8,128)(2,1)}, bf16[4,288,512]{2,1,0:T(8,128)(2,1)}, u32[]{:S(2)}, u32[]{:S(2)}) %collective-permute-start.21) | collective-permute-done | bytes 1179680 | tf_op jit(solution)/shard_map/ppermute | solution.py:452
  232.5 10.9 %last.1 = (f32[1024,256]{1,0:T(8,128)}, f32[4,1024]{1,0:T(4,128)S(1)}) custom-call(s32[4]{0:T(128)S(1)} %copy-done.25, f32[5]{0:T(128)S(1)} %pad_maximum_fusion.scale_ref, bf16[128,9216]{1,0:T(8,128)(2,1)S(1)} %rotate_grad.1.mine_ref, bf16[128,9216]{1,0:T(8,128)(2,1)S(1)} %copy-done.2, bf16[4,288,512]{2,1,0:T(8,128)(2,1)} %collective-permute-done.10.refs_0_, ...), custom_call_target="tpu_custom_call" | custom-call | tf_op jit(solution)/shard_map/last/pallas_call | solution.py:427
  243.7 3.9 %collective-permute-start.26 = (f32[2,128]{1,0:T(2,128)S(1)}, f32[2,128]{1,0:T(2,128)S(1)}, u32[]{:S(2)}, u32[]{:S(2)}) collective-permute-start(f32[2,128]{1,0:T(2,128)S(1)} %div.10), channel_id=1, source_target_pairs={{0,1},{1,0},{2,3},{3,2},{4,5},{5,4},{6,7},{7,6},{8,9},{9,8},{10,11... | collective-permute-start | bytes 3080 | tf_op jit(solution)/shard_map/ppermute | solution.py:511
  248.5 17.2 %all_to_all.10 = f32[128,2,128]{2,1,0:T(2,128)S(1)} all-to-all(f32[128,2,128]{2,1,0:T(2,128)S(1)} %broadcast_in_dim.10), channel_id=1, replica_groups=mesh['dp_0'=4,'dp_1'=4,'dp_2'=4,'mp_0'=2,'mp_1'=2] {'dp_0','dp_1','dp_2'..., dimensions={0} | all-to-all | bytes 262144 | tf_op jit(solution)/shard_map/all_to_all | solution.py:513
  (105 shorter events, 28.5 us)
Async XLA Ops:
  6.2 37.0 %all-to-all-start = ((bf16[16,360,128]{2,1,0:T(8,128)(2,1)}), bf16[16,360,128]{2,1,0:T(8,128)(2,1)S(1)}, u32[]{:S(2)}, u32[]{:S(2)}) async-start(bf16[16,360,128]{2,1,0:T(8,128)(2,1)} %pack.1), calls=%async_computation | async-start | bytes 2949120 | tf_op jit(solution)/shard_map/all_to_all | solution.py:487
  14.0 10.9 %collective-permute-start.5 = (bf16[144,1024]{1,0:T(8,128)(2,1)S(1)}, bf16[144,1024]{1,0:T(8,128)(2,1)S(1)}, u32[]{:S(2)}, u32[]{:S(2)}) collective-permute-start(bf16[144,1024]{1,0:T(8,128)(2,1)S(1)} %copy-done.11), channel_id=1, source_target_pairs={{0,4},{4,8},{8,12},{12,0},{1,5},{5,9},{9,13},{13,1},{2,6},{6,10},{... | collective-permute-start | bytes 884744 | tf_op jit(solution)/shard_map/ppermute | solution.py:452
  15.7 22.9 %collective-permute-start.6 = (bf16[144,1024]{1,0:T(8,128)(2,1)S(1)}, bf16[144,1024]{1,0:T(8,128)(2,1)S(1)}, u32[]{:S(2)}, u32[]{:S(2)}) collective-permute-start(bf16[144,1024]{1,0:T(8,128)(2,1)S(1)} %copy-done.11), channel_id=1, source_target_pairs={{0,8},{4,12},{8,0},{12,4},{1,9},{5,13},{9,1},{13,5},{2,10},{6,14},... | collective-permute-start | bytes 884744 | tf_op jit(solution)/shard_map/ppermute | solution.py:452
  18.7 19.9 %collective-permute-start.7 = (bf16[144,1024]{1,0:T(8,128)(2,1)S(1)}, bf16[144,1024]{1,0:T(8,128)(2,1)S(1)}, u32[]{:S(2)}, u32[]{:S(2)}) collective-permute-start(bf16[144,1024]{1,0:T(8,128)(2,1)S(1)} %copy-done.11), channel_id=1, source_target_pairs={{0,12},{4,0},{8,4},{12,8},{1,13},{5,1},{9,5},{13,9},{2,14},{6,2},{... | collective-permute-start | bytes 884744 | tf_op jit(solution)/shard_map/ppermute | solution.py:452
  39.5 66.5 %copy-start.20 = (bf16[2,288,512]{2,1,0:T(8,128)(2,1)}, bf16[2,288,512]{2,1,0:T(8,128)(2,1)S(1)}, u32[]{:S(2)}) copy-start(bf16[2,288,512]{2,1,0:T(8,128)(2,1)S(1)} %get-tuple-element.25.refs_0_) | copy-start | bytes 1769476
  39.5 14.9 %collective-permute-start.18 = (bf16[2,288,512]{2,1,0:T(8,128)(2,1)S(1)}, bf16[2,288,512]{2,1,0:T(8,128)(2,1)}, u32[]{:S(2)}, u32[]{:S(2)}) collective-permute-start(bf16[2,288,512]{2,1,0:T(8,128)(2,1)S(1)} %get-tuple-element.25.refs_0_), channel_id=1, source_target_pairs={{0,192},{64,0},{128,64},{192,128},{1,193},{65,1},{129,65},{193,129... | collective-permute-start | bytes 1769480 | tf_op jit(solution)/shard_map/ppermute | solution.py:452
  42.1 15.2 %collective-permute-start.15 = (bf16[2,288,512]{2,1,0:T(8,128)(2,1)S(1)}, bf16[2,288,512]{2,1,0:T(8,128)(2,1)S(1)}, u32[]{:S(2)}, u32[]{:S(2)}) collective-permute-start(bf16[2,288,512]{2,1,0:T(8,128)(2,1)S(1)} %get-tuple-element.25.refs_0_), channel_id=1, source_target_pairs={{0,64},{64,128},{128,192},{192,0},{1,65},{65,129},{129,193},{193,1... | collective-permute-start | bytes 1769480 | tf_op jit(solution)/shard_map/ppermute | solution.py:452
  42.1 21.7 %collective-permute-start.8 = (bf16[2,288,512]{2,1,0:T(8,128)(2,1)}, bf16[2,288,512]{2,1,0:T(8,128)(2,1)S(1)}, u32[]{:S(2)}, u32[]{:S(2)}) collective-permute-start(bf16[2,288,512]{2,1,0:T(8,128)(2,1)} %get-tuple-element.24.refs_0_), channel_id=1, source_target_pairs={{0,16},{16,32},{32,48},{48,0},{1,17},{17,33},{33,49},{49,1},{2,18}... | collective-permute-start | bytes 1769480 | tf_op jit(solution)/shard_map/ppermute | solution.py:452
  43.3 67.8 %copy-start.3 = (bf16[16,360,128]{2,1,0:T(8,128)(2,1)}, bf16[16,360,128]{2,1,0:T(8,128)(2,1)S(1)}, u32[]{:S(2)}) copy-start(bf16[16,360,128]{2,1,0:T(8,128)(2,1)S(1)} %all-to-all-done.own_ref) | copy-start | bytes 4423684
  43.3 69.0 %collective-permute-start = (bf16[16,144,128]{2,1,0:T(8,128)(2,1)S(1)}, bf16[16,144,128]{2,1,0:T(8,128)(2,1)S(1)}, u32[]{:S(2)}, u32[]{:S(2)}) collective-permute-start(bf16[16,144,128]{2,1,0:T(8,128)(2,1)S(1)} %slice.8), channel_id=1, source_target_pairs={{0,4},{4,8},{8,12},{12,2},{2,14},{6,0},{10,6},{14,10},{1,5},{5,9},... | collective-permute-start | bytes 1769480 | tf_op jit(solution)/shard_map/ppermute | solution.py:473
  50.0 65.0 %collective-permute-start.1 = (bf16[16,144,128]{2,1,0:T(8,128)(2,1)S(1)}, bf16[16,144,128]{2,1,0:T(8,128)(2,1)S(1)}, u32[]{:S(2)}, u32[]{:S(2)}) collective-permute-start(bf16[16,144,128]{2,1,0:T(8,128)(2,1)S(1)} %slice.8), channel_id=1, source_target_pairs={{0,6},{4,10},{8,14},{12,0},{2,12},{6,2},{10,4},{14,8},{1,7},{5,11}... | collective-permute-start | bytes 1769480 | tf_op jit(solution)/shard_map/ppermute | solution.py:473
  54.4 66.8 %collective-permute-start.12 = (bf16[2,288,512]{2,1,0:T(8,128)(2,1)}, bf16[2,288,512]{2,1,0:T(8,128)(2,1)S(1)}, u32[]{:S(2)}, u32[]{:S(2)}) collective-permute-start(bf16[2,288,512]{2,1,0:T(8,128)(2,1)} %get-tuple-element.24.refs_0_), channel_id=1, source_target_pairs={{0,48},{16,0},{32,16},{48,32},{1,49},{17,1},{33,17},{49,33},{2,50}... | collective-permute-start | bytes 1769480 | tf_op jit(solution)/shard_map/ppermute | solution.py:452
  58.1 47.9 %collective-permute-start.2 = (bf16[16,72,128]{2,1,0:T(8,128)(2,1)S(1)}, bf16[16,72,128]{2,1,0:T(8,128)(2,1)S(1)}, u32[]{:S(2)}, u32[]{:S(2)}) collective-permute-start(bf16[16,72,128]{2,1,0:T(8,128)(2,1)S(1)} %slice.9), channel_id=1, source_target_pairs={{0,8},{4,12},{8,2},{12,6},{2,10},{6,14},{10,0},{14,4},{1,9},{5,13}... | collective-permute-start | bytes 884744 | tf_op jit(solution)/shard_map/ppermute | solution.py:473
  63.8 48.4 %collective-permute-start.3 = (bf16[16,72,128]{2,1,0:T(8,128)(2,1)S(1)}, bf16[16,72,128]{2,1,0:T(8,128)(2,1)S(1)}, u32[]{:S(2)}, u32[]{:S(2)}) collective-permute-start(bf16[16,72,128]{2,1,0:T(8,128)(2,1)S(1)} %slice.9), channel_id=1, source_target_pairs={{0,10},{4,14},{8,0},{12,4},{2,8},{6,12},{10,2},{14,6},{1,11},{5,15... | collective-permute-start | bytes 884744 | tf_op jit(solution)/shard_map/ppermute | solution.py:473
  106.0 17.0 %collective-permute-start.19 = (bf16[2,288,512]{2,1,0:T(8,128)(2,1)}, bf16[2,288,512]{2,1,0:T(8,128)(2,1)S(1)}, u32[]{:S(2)}, u32[]{:S(2)}) collective-permute-start(bf16[2,288,512]{2,1,0:T(8,128)(2,1)} %collective-permute-done.18.refs_1_), channel_id=1, source_target_pairs={{0,192},{64,0},{128,64},{192,128},{1,193},{65,1},{129,65},{193,129... | collective-permute-start | bytes 1769480 | tf_op jit(solution)/shard_map/ppermute | solution.py:452
  112.2 45.8 %collective-permute-start.9 = (bf16[4,288,512]{2,1,0:T(8,128)(2,1)S(1)}, bf16[4,288,512]{2,1,0:T(8,128)(2,1)}, u32[]{:S(2)}, u32[]{:S(2)}) collective-permute-start(bf16[4,288,512]{2,1,0:T(8,128)(2,1)S(1)} %join.4.p_ref), channel_id=1, source_target_pairs={{0,64},{64,128},{128,192},{192,0},{1,65},{65,129},{129,193},{193,1... | collective-permute-start | bytes 3538952 | tf_op jit(solution)/shard_map/ppermute | solution.py:452
  112.4 45.7 %collective-permute-start.22 = (bf16[4,288,512]{2,1,0:T(8,128)(2,1)S(1)}, bf16[4,288,512]{2,1,0:T(8,128)(2,1)S(1)}, u32[]{:S(2)}, u32[]{:S(2)}) collective-permute-start(bf16[4,288,512]{2,1,0:T(8,128)(2,1)S(1)} %join.4.p_ref), channel_id=1, source_target_pairs={{0,192},{64,0},{128,64},{192,128},{1,193},{65,1},{129,65},{193,129... | collective-permute-start | bytes 3538952 | tf_op jit(solution)/shard_map/ppermute | solution.py:452
  115.0 40.3 %collective-permute-start.16 = (bf16[4,288,512]{2,1,0:T(8,128)(2,1)S(1)}, bf16[4,288,512]{2,1,0:T(8,128)(2,1)}, u32[]{:S(2)}, u32[]{:S(2)}) collective-permute-start(bf16[4,288,512]{2,1,0:T(8,128)(2,1)S(1)} %join.6.p_ref), channel_id=1, source_target_pairs={{0,16},{16,32},{32,48},{48,0},{1,17},{17,33},{33,49},{49,1},{2,18}... | collective-permute-start | bytes 3538952 | tf_op jit(solution)/shard_map/ppermute | solution.py:452
  121.3 66.5 %collective-permute-start.4 = (bf16[128,9216]{1,0:T(8,128)(2,1)S(1)}, bf16[128,9216]{1,0:T(8,128)(2,1)S(1)}, u32[]{:S(2)}, u32[]{:S(2)}) collective-permute-start(bf16[128,9216]{1,0:T(8,128)(2,1)S(1)} %rotate_grad.1.mine_ref), channel_id=1, source_target_pairs={{0,1},{1,0},{2,3},{3,2},{4,5},{5,4},{6,7},{7,6},{8,9},{9,8},{10,11... | collective-permute-start | bytes 7077896 | tf_op jit(solution)/shard_map/ppermute | solution.py:491
  123.0 32.0 %collective-permute-start.11 = (bf16[2,288,512]{2,1,0:T(8,128)(2,1)S(1)}, bf16[2,288,512]{2,1,0:T(8,128)(2,1)S(1)}, u32[]{:S(2)}, u32[]{:S(2)}) collective-permute-start(bf16[2,288,512]{2,1,0:T(8,128)(2,1)S(1)} %copy-done.19), channel_id=1, source_target_pairs={{0,16},{16,32},{32,48},{48,0},{1,17},{17,33},{33,49},{49,1},{2,18}... | collective-permute-start | bytes 1769480 | tf_op jit(solution)/shard_map/ppermute | solution.py:452
  125.2 62.6 %copy-start.7 = (bf16[4,288,512]{2,1,0:T(8,128)(2,1)}, bf16[4,288,512]{2,1,0:T(8,128)(2,1)S(1)}, u32[]{:S(2)}) copy-start(bf16[4,288,512]{2,1,0:T(8,128)(2,1)S(1)} %join.7.q_ref) | copy-start | bytes 3538948
  125.2 65.2 %copy-start.25 = (s32[4]{0:T(128)S(1)}, s32[4]{0:T(128)}, u32[]{:S(2)}) copy-start(s32[4]{0:T(128)} %len_ref.15) | copy-start | bytes 52
  155.1 26.5 %collective-permute-start.25 = (bf16[4,288,512]{2,1,0:T(8,128)(2,1)S(1)}, bf16[4,288,512]{2,1,0:T(8,128)(2,1)S(1)}, u32[]{:S(2)}, u32[]{:S(2)}) collective-permute-start(bf16[4,288,512]{2,1,0:T(8,128)(2,1)S(1)} %join.7.q_ref), channel_id=1, source_target_pairs={{0,16},{16,32},{32,48},{48,0},{1,17},{17,33},{33,49},{49,1},{2,18}... | collective-permute-start | bytes 3538952 | tf_op jit(solution)/shard_map/ppermute | solution.py:452
  155.3 27.3 %collective-permute-start.20 = (bf16[4,288,512]{2,1,0:T(8,128)(2,1)S(1)}, bf16[4,288,512]{2,1,0:T(8,128)(2,1)}, u32[]{:S(2)}, u32[]{:S(2)}) collective-permute-start(bf16[4,288,512]{2,1,0:T(8,128)(2,1)S(1)} %join.7.q_ref), channel_id=1, source_target_pairs={{0,48},{16,0},{32,16},{48,32},{1,49},{17,1},{33,17},{49,33},{2,50}... | collective-permute-start | bytes 3538952 | tf_op jit(solution)/shard_map/ppermute | solution.py:452
  158.1 26.0 %collective-permute-start.23 = (bf16[4,288,512]{2,1,0:T(8,128)(2,1)S(1)}, bf16[4,288,512]{2,1,0:T(8,128)(2,1)S(1)}, u32[]{:S(2)}, u32[]{:S(2)}) collective-permute-start(bf16[4,288,512]{2,1,0:T(8,128)(2,1)S(1)} %join.5.q_ref), channel_id=1, source_target_pairs={{0,64},{64,128},{128,192},{192,0},{1,65},{65,129},{129,193},{193,1... | collective-permute-start | bytes 3538952 | tf_op jit(solution)/shard_map/ppermute | solution.py:452
  159.1 26.0 %collective-permute-start.13 = (bf16[4,288,512]{2,1,0:T(8,128)(2,1)S(1)}, bf16[4,288,512]{2,1,0:T(8,128)(2,1)}, u32[]{:S(2)}, u32[]{:S(2)}) collective-permute-start(bf16[4,288,512]{2,1,0:T(8,128)(2,1)S(1)} %join.5.q_ref), channel_id=1, source_target_pairs={{0,192},{64,0},{128,64},{192,128},{1,193},{65,1},{129,65},{193,129... | collective-permute-start | bytes 3538952 | tf_op jit(solution)/shard_map/ppermute | solution.py:452
  182.6 31.0 %collective-permute-start.24 = (bf16[4,288,512]{2,1,0:T(8,128)(2,1)S(1)}, bf16[4,288,512]{2,1,0:T(8,128)(2,1)}, u32[]{:S(2)}, u32[]{:S(2)}) collective-permute-start(bf16[4,288,512]{2,1,0:T(8,128)(2,1)S(1)} %join.6.p_ref), channel_id=1, source_target_pairs={{0,48},{16,0},{32,16},{48,32},{1,49},{17,1},{33,17},{49,33},{2,50}... | collective-permute-start | bytes 3538952 | tf_op jit(solution)/shard_map/ppermute | solution.py:452
  182.6 35.7 %collective-permute-start.10 = (bf16[4,288,512]{2,1,0:T(8,128)(2,1)}, bf16[4,288,512]{2,1,0:T(8,128)(2,1)}, u32[]{:S(2)}, u32[]{:S(2)}) collective-permute-start(bf16[4,288,512]{2,1,0:T(8,128)(2,1)} %collective-permute-done.9.p_ref), channel_id=1, source_target_pairs={{0,64},{64,128},{128,192},{192,0},{1,65},{65,129},{129,193},{193,1... | collective-permute-start | bytes 3538952 | tf_op jit(solution)/shard_map/ppermute | solution.py:452
  185.1 33.2 %collective-permute-start.17 = (bf16[4,288,512]{2,1,0:T(8,128)(2,1)}, bf16[4,288,512]{2,1,0:T(8,128)(2,1)}, u32[]{:S(2)}, u32[]{:S(2)}) collective-permute-start(bf16[4,288,512]{2,1,0:T(8,128)(2,1)} %collective-permute-done.16.p_ref), channel_id=1, source_target_pairs={{0,16},{16,32},{32,48},{48,0},{1,17},{17,33},{33,49},{49,1},{2,18}... | collective-permute-start | bytes 3538952 | tf_op jit(solution)/shard_map/ppermute | solution.py:452
  185.1 47.4 %collective-permute-start.21 = (bf16[4,288,512]{2,1,0:T(8,128)(2,1)}, bf16[4,288,512]{2,1,0:T(8,128)(2,1)}, u32[]{:S(2)}, u32[]{:S(2)}) collective-permute-start(bf16[4,288,512]{2,1,0:T(8,128)(2,1)} %collective-permute-done.20.q_ref), channel_id=1, source_target_pairs={{0,48},{16,0},{32,16},{48,32},{1,49},{17,1},{33,17},{49,33},{2,50}... | collective-permute-start | bytes 3538952 | tf_op jit(solution)/shard_map/ppermute | solution.py:452
  189.2 43.3 %collective-permute-start.14 = (bf16[4,288,512]{2,1,0:T(8,128)(2,1)}, bf16[4,288,512]{2,1,0:T(8,128)(2,1)}, u32[]{:S(2)}, u32[]{:S(2)}) collective-permute-start(bf16[4,288,512]{2,1,0:T(8,128)(2,1)} %collective-permute-done.13.q_ref), channel_id=1, source_target_pairs={{0,192},{64,0},{128,64},{192,128},{1,193},{65,1},{129,65},{193,129... | collective-permute-start | bytes 3538952 | tf_op jit(solution)/shard_map/ppermute | solution.py:452
  243.7 4.7 %collective-permute-start.26 = (f32[2,128]{1,0:T(2,128)S(1)}, f32[2,128]{1,0:T(2,128)S(1)}, u32[]{:S(2)}, u32[]{:S(2)}) collective-permute-start(f32[2,128]{1,0:T(2,128)S(1)} %div.10), channel_id=1, source_target_pairs={{0,1},{1,0},{2,3},{3,2},{4,5},{5,4},{6,7},{7,6},{8,9},{9,8},{10,11... | collective-permute-start | bytes 3080 | tf_op jit(solution)/shard_map/ppermute | solution.py:511
  (22 other events, 127.1 us)
